TPU v7x, 256 devices: a whole 4x4x8 slice. The times are simulated.
256 devices in a mesh: row: 16 (over y_hi, x, core), col: 16 (over z, y_lo).
Axes of the slice: x: 4, y: 4 (y_hi: 2, y_lo: 2; y = y_hi * 2 + y_lo), z: 8, core: 2. Of those that a mesh axis runs over, the one named last changes fastest.
Arguments:
- queries: bfloat16 [2048, 3072], P('row'), may hold values from -30 to 30
- latent_pool: bfloat16 [512, 64, 576], P('col'), may hold values from -6 to 6
- block_table: int32 [512], P('col'), may hold values from 0 to 31, as said below
- page_len: int32 [512], P('col'), may hold values from 16 to 64
- group_offset: int32 [1], replicated, may hold values from 0 to 30720
- hidden: bfloat16 [2048, 2048], P('row'), may hold values from -4 to 4
- latent_up: bfloat16 [512, 4096], replicated, may hold values from -0.25 to 0.25
- output_weight: bfloat16 [2048, 2048], P('col'), may hold values from -0.1875 to 0.1875
- gate_weight: bfloat16 [2048, 10944], P('row', 'col'), may hold values from -0.125 to 0.125
- up_weight: bfloat16 [2048, 10944], P('row', 'col'), may hold values from -0.125 to 0.125
- down_weight: bfloat16 [10944, 2048], P('col', 'row'), may hold values from -0.078125 to 0.078125
Outputs:
- attended: bfloat16 [2048, 2048], P('row')
- block_out: bfloat16 [2048, 2048], P('row', 'col')
Inputs may be any that keep to these rules, and one draw needn't show every extreme that they name: `block_table`: the 32 logical pages of one col index name its 32 pool pages, each once.
All inputs are finite; a program needn't handle non-finite values.
Results may differ from a plain program's by a relative error of at most 0.015.
Values may be sent and summed in bfloat16 or wider, within the bound.
A program may use at most 128 MiB of HBM per device.

v0:
```python
import math

import jax
import jax.numpy as jnp
from jax import lax
from jax.sharding import PartitionSpec as P

H = 16
NOPE = 128
VDIM = 128
LATENT = 512
QK = 192


def joined(x, axis, combine):
    everything = jax.tree.map(lambda part: lax.all_gather(part, axis), x)
    first = jax.tree.map(lambda part: part[0], everything)

    def step(k, so_far):
        return combine(so_far, jax.tree.map(lambda part: part[k], everything))

    return lax.fori_loop(1, lax.axis_size(axis), step, first)


def join_partials(left_part, right_part):
    left_max, left_total, left_out = left_part
    right_max, right_total, right_out = right_part
    row_max = jnp.maximum(left_max, right_max)
    left_weight = jnp.exp(left_max - row_max)
    right_weight = jnp.exp(right_max - row_max)
    totals = left_weight * left_total + right_weight * right_total
    outputs = left_weight[..., None] * left_out + right_weight[..., None] * right_out
    return (row_max, totals, outputs)


def on_device(
    queries,
    latent_pool,
    block_table,
    page_len,
    group_offset,
    hidden,
    latent_up,
    output_weight,
    gate_weight,
    up_weight,
    down_weight,
):
    col_count = lax.axis_size("col")
    col_index = lax.axis_index("col")
    row_index = lax.axis_index("row")
    query_rows = queries.shape[0]
    page_count, page_size, cache_width = latent_pool.shape
    key_count = page_count * page_size
    latent = latent_pool[block_table].reshape(key_count, cache_width)
    key_index = jnp.arange(key_count, dtype=jnp.int32)
    positions = col_index * key_count + key_index
    lengths = jnp.broadcast_to(page_len[:, None], (page_count, page_size)).reshape(key_count)
    key_valid = key_index % page_size < lengths
    query_pos = group_offset[0] + row_index * query_rows + jnp.arange(query_rows, dtype=jnp.int32)
    visible = key_valid[None, :] & (positions[None, :] <= query_pos[:, None])
    latent_part = latent[:, :LATENT]
    rope_keys = latent[:, LATENT:]
    per_head = queries.reshape(query_rows, H, QK)
    score_scale = 1.0 / math.sqrt(QK)

    def one_head(head_index):
        columns = lax.dynamic_slice_in_dim(latent_up, head_index * (NOPE + VDIM), NOPE + VDIM, 1)
        expanded = jnp.dot(latent_part, columns, preferred_element_type=jnp.float32).astype(
            jnp.bfloat16
        )
        key_rows = jnp.concatenate([expanded[:, :NOPE], rope_keys], axis=1)
        values = expanded[:, NOPE:]
        head_queries = lax.dynamic_index_in_dim(per_head, head_index, 1, keepdims=False)
        scores = jnp.dot(head_queries, key_rows.T, preferred_element_type=jnp.float32) * score_scale
        row_max = jnp.max(jnp.where(visible, scores, -1e30), axis=1)
        weights = jnp.where(visible, jnp.exp(scores - row_max[:, None]), 0.0)
        totals = jnp.sum(weights, axis=1)
        outputs = jnp.dot(weights.astype(jnp.bfloat16), values, preferred_element_type=jnp.float32)
        return (row_max, totals, outputs)

    head_max, head_total, head_out = lax.map(one_head, jnp.arange(H, dtype=jnp.int32))
    heads_here = H // col_count
    out_rows = output_weight.reshape(heads_here, VDIM, output_weight.shape[1])
    merged_max, merged_total, merged_out = joined(
        (head_max, head_total, head_out), "col", join_partials
    )
    mine_out = lax.dynamic_slice_in_dim(merged_out, col_index * heads_here, heads_here, 0)
    mine_total = lax.dynamic_slice_in_dim(merged_total, col_index * heads_here, heads_here, 0)
    head_mix = (mine_out / mine_total[..., None]).astype(jnp.bfloat16)
    partial_value = jnp.einsum(
        "hqv,hvd->qd", head_mix, out_rows, preferred_element_type=jnp.float32
    )
    width_here = hidden.shape[1] // col_count
    projected = lax.psum(partial_value, "col")
    attended = (hidden.astype(jnp.float32) + projected).astype(jnp.bfloat16)
    wide = attended.astype(jnp.float32)
    mean_square = jnp.mean(wide * wide, axis=1, keepdims=True)
    normed = (wide * lax.rsqrt(mean_square + 1e-06)).astype(jnp.bfloat16)
    gate_piece = lax.all_gather(gate_weight, "row", axis=0, tiled=True)
    up_piece = lax.all_gather(up_weight, "row", axis=0, tiled=True)
    gate_next = jnp.dot(normed, gate_piece, preferred_element_type=jnp.float32)
    up_next = jnp.dot(normed, up_piece, preferred_element_type=jnp.float32)
    activated = (jax.nn.silu(gate_next) * up_next).astype(jnp.bfloat16)
    mlp_terms = jnp.dot(
        activated,
        lax.all_gather(down_weight, "row", axis=1, tiled=True),
        preferred_element_type=jnp.float32,
    )
    mlp_share = lax.psum_scatter(mlp_terms, "col", scatter_dimension=1, tiled=True)
    attended_part = lax.dynamic_slice_in_dim(wide, col_index * width_here, width_here, 1)
    block_out = (attended_part + mlp_share).astype(jnp.bfloat16)
    return (attended, block_out)


def solution(mesh):
    placed = (
        P("row", None),
        P("col", None, None),
        P("col"),
        P("col"),
        P(),
        P("row", None),
        P(),
        P("col", None),
        P("row", "col"),
        P("row", "col"),
        P("col", "row"),
    )
    return jax.shard_map(
        on_device,
        mesh=mesh,
        in_specs=placed,
        out_specs=(P("row", None), P("row", "col")),
        check_vma=False,
    )
```

profile of v0, /device:TPU:1, one launch (start us, length us, event | category | flops | bytes accessed | tf_op | source)
XLA Modules:
  0.0 861.0 jit_solution(16877968339074296662)
XLA Ops:
  12.1 3.1 slice.35
  19.7 170.1 %while.35 = (s32[]{:T(128)}, f32[16,128]{1,0:T(8,128)S(1)}, f32[16,128]{1,0:T(8,128)S(1)}, f32[16,128,128]{2,1,0:T(8,128)}, s32[16]{0:T(128)S(1)}, /*index=5*/bf...) while((s32[]{:T(128)}, f32[16,128]{1,0:T(8,128)S(1)}, ...), condition=%wide.region_3.4_spmd.clone, body=%wide.region_0.3_spmd.clone.sunk | while | flops 710672128 | bytes 13259045 | solution.py:82
  42.2 2.5 fusion.66
  52.8 2.5 fusion.66
  63.5 2.5 fusion.66
  74.1 2.5 fusion.66
  106.0 2.5 fusion.66
  189.8 38.7 %all-gather = f32[256,128]{1,0:T(8,128)S(1)} all-gather(f32[16,128]{1,0:T(8,128)S(1)} %get-tuple-element.233), channel_id=2, replica_groups=mesh['row'=16,'col'=16] {'col'}, dimensions={0}, use_global_device_ids=true | all-gather | bytes 139264 | tf_op jit(solution)/shard_map/all_gather | solution.py:16
  228.6 37.3 %all-gather.1 = f32[256,128]{1,0:T(8,128)S(1)} all-gather(f32[16,128]{1,0:T(8,128)S(1)} %get-tuple-element.234), channel_id=3, replica_groups=mesh['row'=16,'col'=16] {'col'}, dimensions={0}, use_global_device_ids=true | all-gather | bytes 139264 | tf_op jit(solution)/shard_map/all_gather | solution.py:16
  265.8 283.1 %all-gather.14.cloned.1.call-done = f32[256,128,128]{2,1,0:T(8,128)} async-done(((f32[16,128,128]{2,1,0:T(8,128)}), f32[256,128,128]{2,1,0:T(8,128)}) %all-gather.14.cloned.1.call-update) | async-done | bytes 16777232 | tf_op jit(solution)/shard_map/all_gather | solution.py:16
  551.2 47.4 %while.34 = (s32[]{:T(128)}, f32[16,128]{1,0:T(8,128)S(1)}, f32[16,128]{1,0:T(8,128)S(1)}, f32[16,128,128]{2,1,0:T(8,128)}, f32[16,16,128]{2,1,0:T(8,128)S(1)}, ...) while((s32[]{:T(128)}, f32[16,128]{1,0:T(8,128)S(1)}, ...), condition=%wide.region_5.6_spmd, body=%wide.region_4.5_spmd.sunk | while | flops 798725 | bytes 3227799 | solution.py:22
  551.2 3.2 fusion.61
  554.4 3.1 fusion.61
  557.6 3.1 fusion.61
  560.8 3.1 fusion.61
  563.9 3.1 fusion.61
  567.1 3.1 fusion.61
  570.2 3.1 fusion.61
  573.4 3.1 fusion.61
  576.5 3.1 fusion.61
  579.7 3.1 fusion.61
  582.8 3.1 fusion.61
  586.0 3.1 fusion.61
  589.1 3.1 fusion.61
  592.3 3.1 fusion.61
  595.4 3.1 fusion.61
  602.7 146.7 %all-reduce.2.cloned.1.call-done = f32[128,2048]{1,0:T(8,128)} async-done(((f32[128,2048]{1,0:T(8,128)}), f32[128,2048]{1,0:T(8,128)}) %all-reduce.2.cloned.1.call-update) | async-done | bytes 1048592 | tf_op jit(solution)/shard_map/psum | solution.py:95
  749.4 2.6 fusion.45
  752.2 2.8 fusion.33
  755.0 31.1 %all-gather.12.cloned.1.call-done = bf16[684,2048]{1,0:T(8,128)(2,1)} async-done(((bf16[684,128]{1,0:T(8,128)(2,1)}), bf16[684,2048]{1,0:T(8,128)(2,1)}) %all-gather.12.cloned.1.call-update) | async-done | bytes 2801680 | tf_op jit(solution)/shard_map/all_gather | solution.py:107
  786.1 5.9 fusion.27
  792.0 60.2 %reduce-scatter.2.cloned.1.call-done = f32[128,128]{1,0:T(8,128)} async-done(((f32[128,2048]{1,0:T(8,128)}), f32[128,128]{1,0:T(8,128)}) %reduce-scatter.2.cloned.1.call-update) | async-done | bytes 65552 | tf_op jit(solution)/shard_map/reduce_scatter | solution.py:110
  (215 shorter events, 131.8 us)
Async XLA Ops:
  8.0 1.8 copy-start
  8.0 540.9 %all-gather.14.cloned.1.call-start = ((), (), s32[]{:S(2)}) async-start(), calls=%async_computation.6 | async-start | bytes 17825792 | tf_op jit(solution)/shard_map/all_gather | solution.py:16
  12.1 7.4 copy-start.4
  23.4 1.0 copy-start.1
  34.0 1.0 copy-start.1
  44.7 1.0 copy-start.1
  55.3 1.0 copy-start.1
  65.9 1.0 copy-start.1
  76.6 1.0 copy-start.1
  87.2 1.0 copy-start.1
  97.8 1.0 copy-start.1
  108.4 1.0 copy-start.1
  119.1 1.0 copy-start.1
  129.7 1.0 copy-start.1
  140.3 1.0 copy-start.1
  150.9 1.0 copy-start.1
  161.6 1.0 copy-start.1
  172.2 1.0 copy-start.1
  182.9 1.0 copy-start.1
  189.8 559.6 %all-reduce.2.cloned.1.call-start = ((), (), s32[]{:S(2)}) async-start(), calls=%async_computation.1 | async-start | bytes 2097152 | tf_op jit(solution)/shard_map/psum | solution.py:95
  551.2 47.4 %copy-start.3 = (bf16[128,2048]{1,0:T(8,128)(2,1)S(1)}, bf16[128,2048]{1,0:T(8,128)(2,1)}, u32[]{:S(2)}) copy-start(bf16[128,2048]{1,0:T(8,128)(2,1)} %param.22) | copy-start | bytes 1572868
  600.9 151.3 %all-gather.8.cloned.1.call-start = ((), (), s32[]{:S(2)}) async-start(), calls=%async_computation.2 | async-start | bytes 2994176 | tf_op jit(solution)/shard_map/all_gather | solution.py:100
  601.4 153.5 %all-gather.10.cloned.1.call-start = ((), (), s32[]{:S(2)}) async-start(), calls=%async_computation.3 | async-start | bytes 2994176 | tf_op jit(solution)/shard_map/all_gather | solution.py:101
  602.0 184.1 %all-gather.12.cloned.1.call-start = ((), (), s32[]{:S(2)}) async-start(), calls=%async_computation.4 | async-start | bytes 2994176 | tf_op jit(solution)/shard_map/all_gather | solution.py:107
  602.6 249.6 %reduce-scatter.2.cloned.1.call-start = ((), (), s32[]{:S(2)}) async-start(), calls=%async_computation.5 | async-start | bytes 1114112 | tf_op jit(solution)/shard_map/reduce_scatter | solution.py:110
  752.0 40.0 %copy-start.2 = (bf16[128,2048]{1,0:T(8,128)(2,1)}, bf16[128,2048]{1,0:T(8,128)(2,1)S(1)}, u32[]{:S(2)}) copy-start(bf16[128,2048]{1,0:T(8,128)(2,1)S(1)} %get-tuple-element.346) | copy-start | bytes 1572868
Sparse Core Ops, SparseCore 0:
  189.9 358.9 all-gather.13
  601.0 148.3 all-reduce.1
  792.1 60.0 reduce-scatter.1
Sparse Core Ops, SparseCore 1:
  603.9 64.6 all-gather.7
  671.0 56.8 all-gather.9
  730.3 55.7 all-gather.11
where the time goes:
time: 875 us; the launch traced here: 861 us
  waiting for transfers between devices  523 us (60%)
  matrix products  105 us (12%)
  blocking collectives  76 us (9%)
  other arithmetic  59.6 us (7%)
  loops' own time  42.2 us (5%)
  local copies, waits for them, and re-layouts  38.9 us (4%)
  between operations  16.2 us (2%)
    all_gather x1, waiting for transfers between devices, joined(): everything = jax.tree.map(lambda part: lax.all_gather(part, axis), x)  283 us
    psum x1, waiting for transfers between devices, on_device(): projected = lax.psum(partial_value, 'col')  147 us
    all_gather x2, blocking collectives, joined(): everything = jax.tree.map(lambda part: lax.all_gather(part, axis), x)  76 us
    reduce_scatter x1, waiting for transfers between devices, on_device(): lax.psum_scatter(mlp_terms, 'col', scatter_dimension=1, tiled=True)  60.2 us
    add x15, other arithmetic, join_partials(): left_weight[..., None] * left_out + right_weight[..., None] * right_out  47.1 us
    another operation x1, loops' own time, on_device(): lax.map(one_head, jnp.arange(H, dtype=jnp.int32))  42.2 us
    dot_general x16, matrix products, one_head(): jnp.dot(latent_part, columns, preferred_element_type=jnp.float32)  39.3 us
    dot_general x16, matrix products, one_head(): jnp.dot(weights.astype(jnp.bfloat16), values, preferred_element_type=jnp....  34.1 us
  transfers between devices with their start and end apart: 6, of which 4 were waited for; matrix products, arithmetic and copies ran while one was open for 1% of the time, Pallas kernels for 0%

commit v1 on v0

v1 whole, which is shorter than its diff:
```python
import functools
import math

import jax
import jax.numpy as jnp
from jax import lax
from jax.experimental import pallas as pl
from jax.experimental.pallas import tpu as pltpu
from jax.sharding import PartitionSpec as P

H = 16
NOPE = 128
ROPE = 64
VDIM = 128
LATENT = 512
QK = 192
MESH = pl.DeviceIdType.MESH
LOW = -1e30
FAR = 1 << 30
SCALE2 = math.log2(math.e) / math.sqrt(QK)
F32 = jnp.float32
BF16 = jnp.bfloat16
YP, XP, XM, SIB, DN = range(5)
KEY_CHUNK = 256


def dot(a, b):
    return jnp.dot(a, b, preferred_element_type=F32)


def dot_nt(a, b):
    return lax.dot_general(a, b, (((1,), (1,)), ((), ())), preferred_element_type=F32)


def kernel(
    ncol, nx,
    q_h, pool_h, table_s, plen_s, off_s, hid_h, lup_h, wo_h, g_h, u_h, d_h,
    att_o, blk_o,
    lat, lupv, qv, hid, wo, gv, uv, dv, keys, vals, sc, kpos,
    o_send, o_recv, st_send, st_recv, p1_send, p1_recv, att, p2_send, p2_recv, act, blk,
    lsem, lup_sem, own_sem, out_sem, ws_sem, wr_sem,
    o_ss, o_rs, st_ss, st_rs, p1_ss, p1_rs, at_ss, at_rs, p2_ss, p2_rs,
):
    row, col = lax.axis_index("row"), lax.axis_index("col")

    def rem(a, b):
        return a % b

    def div(a, b):
        return a // b

    core, x, yhi = rem(row, 2), rem(div(row, 2), nx), div(row, 2 * nx)

    def row_of(yy, xx, cc):
        return (yy * nx + xx) * 2 + cc

    xp, xm, x2 = rem(x + 1, nx), rem(x + nx - 1, nx), rem(x + 2, nx)
    yo, co = 1 - yhi, 1 - core
    plus = [xp, xm, jnp.where(core == 0, xp, xm)]
    minus = [xm, xp, jnp.where(core == 0, xm, xp)]
    peers = [row_of(yo, x, core), row_of(yhi, xp, core), row_of(yhi, xm, core), row_of(yhi, x, co)]
    ups = [[row_of(yy, minus[t], core) for t in range(3)] for yy in (yhi, yo)]
    dns = [[row_of(yy, plus[t], core) for t in range(3)] for yy in (yhi, yo)]
    x2s = [row_of(yy, x2, core) for yy in (yhi, yo)]
    full = [gv, uv, dv]
    mine_h = [g_h, u_h, d_h]

    pairs = H // 2
    first_pair = div(col, 2) + 1
    loads = [
        pltpu.make_async_copy(pool_h, lat, lsem.at[0]),
        pltpu.make_async_copy(q_h, qv, lsem.at[1]),
        pltpu.make_async_copy(wo_h, wo, lsem.at[2]),
        pltpu.make_async_copy(hid_h.at[:, pl.ds(pl.multiple_of(col * 128, 128), 128)], hid, lsem.at[3]),
    ]

    def lup_load(i):
        p = rem(first_pair + i, pairs)
        return pltpu.make_async_copy(
            lup_h.at[:, pl.ds(pl.multiple_of(p * 512, 512), 512)], lupv.at[p], lup_sem.at[i]
        )

    loads[0].start()
    lup_load(0).start()
    loads[1].start()

    barrier = pltpu.get_barrier_semaphore()

    @pl.loop(1, ncol)
    def _(t):
        pl.semaphore_signal(barrier, inc=1, device_id=(row, rem(col + t, ncol)), device_id_type=MESH)

    for peer in peers:
        pl.semaphore_signal(barrier, inc=1, device_id=(peer, col), device_id_type=MESH)

    for i in range(1, pairs):
        lup_load(i).start()
    own_loads = [pltpu.make_async_copy(mine_h[t], full[t].at[row], own_sem.at[t]) for t in range(3)]
    loads[2].start()
    loads[3].start()
    for c in own_loads:
        c.start()

    base = col * kpos.shape[1]
    lane = lax.broadcasted_iota(jnp.int32, kpos.shape, 1)
    page, slot = lax.shift_right_logical(lane, 6), lane & 63
    kp = jnp.full(kpos.shape, FAR, jnp.int32)
    for p in range(lat.shape[0]):
        here = jnp.where(slot < plen_s[p], base + p * 64 + slot, FAR)
        kp = jnp.where(page == table_s[p], here, kp)
    kpos[...] = kp
    qpos = off_s[0] + row * 128 + lax.broadcasted_iota(jnp.int32, (128, 1), 0)

    pl.semaphore_wait(barrier, ncol - 1 + len(peers))

    sent = []

    def wcopy(t, owner, kind, dest, source=None):
        return pltpu.make_async_remote_copy(
            src_ref=full[t].at[owner] if source is None else source,
            dst_ref=full[t].at[owner],
            send_sem=ws_sem.at[t, kind, owner],
            recv_sem=wr_sem.at[t, owner],
            device_id=(dest, col),
            device_id_type=MESH,
        )

    def wsend(t, owner, kind, dest, source=None):
        wcopy(t, owner, kind, dest, source).start()
        sent.append((t, owner, kind, dest, source))

    def warrive(t, owner):
        wcopy(t, owner, SIB, peers[SIB]).wait_recv()

    def stage_own(t):
        for kind in range(4):
            wsend(t, row, kind, peers[kind], mine_h[t])

    def stage_y(t):
        o = peers[YP]
        warrive(t, o)
        for kind in (XP, XM, SIB):
            wsend(t, o, kind, peers[kind])

    def stage_x(t, yy):
        up, dn = ups[yy][t], dns[yy][t]
        warrive(t, up)
        wsend(t, up, DN, dns[0][t])
        wsend(t, up, SIB, peers[SIB])
        warrive(t, dn)
        wsend(t, dn, SIB, peers[SIB])

    def stage_x2(t, yy):
        o = x2s[yy]
        warrive(t, o)
        wsend(t, o, SIB, peers[SIB])

    def stage_sib(t):
        for yy in range(2):
            for xx in range(nx):
                warrive(t, row_of(yy, xx, co))

    stage_own(0)
    stage_own(1)

    schedule = {
        3: [lambda: stage_x(0, 0), lambda: stage_x(1, 0)],
        5: [lambda: stage_y(0), lambda: stage_y(1), lambda: stage_own(2)],
    }

    loads[0].wait()
    zeros64 = jnp.zeros((keys.shape[1], 64), BF16)
    rope = lat[:, :, LATENT:].reshape(keys.shape[1], ROPE)
    for hh in range(2):
        keys[hh, :, NOPE:] = jnp.concatenate([rope, zeros64], axis=1)
    loads[1].wait()
    nkeys = keys.shape[1]

    def o_copy(head):
        return (
            pltpu.make_async_remote_copy(
                src_ref=o_send.at[head], dst_ref=o_recv.at[col], send_sem=o_ss.at[head],
                recv_sem=o_rs.at[col], device_id=(row, head), device_id_type=MESH),
            pltpu.make_async_remote_copy(
                src_ref=st_send.at[head], dst_ref=st_recv.at[col], send_sem=st_ss.at[head],
                recv_sem=st_rs.at[col], device_id=(row, head), device_id_type=MESH),
        )

    lane128 = lax.broadcasted_iota(jnp.int32, (128, 128), 1)

    @pl.loop(0, pairs)
    def _(i):
        p = rem(first_pair + i, pairs)
        pltpu.make_async_copy(lup_h.at[:, pl.ds(0, 512)], lupv.at[p], lup_sem.at[i]).wait()
        w = lupv[p]
        for kc in range(4):
            rows = slice(kc * 512, (kc + 1) * 512)
            e = dot(lat[kc * 8:(kc + 1) * 8, :, :LATENT].reshape(512, LATENT), w).astype(BF16)
            keys[0, rows, :NOPE] = e[:, :128]
            vals[0, rows, :] = e[:, 128:256]
            keys[1, rows, :NOPE] = e[:, 256:384]
            vals[1, rows, :] = e[:, 384:]
        qp = qv[:, pl.ds(pl.multiple_of(p * 2 * QK, 2 * QK), 2 * QK)]
        zq = jnp.zeros((128, 64), BF16)
        for hh in range(2):
            q = jnp.concatenate([qp[:, hh * QK:(hh + 1) * QK], zq], axis=1)
            best = jnp.full((128, 128), LOW, F32)
            for kc in range(nkeys // KEY_CHUNK):
                ks = slice(kc * KEY_CHUNK, (kc + 1) * KEY_CHUNK)
                s = dot_nt(q, keys[hh, ks, :])
                s = jnp.where(kpos[:, ks] <= qpos, s, LOW)
                sc[hh, :, ks] = s
                for j in range(KEY_CHUNK // 128):
                    best = jnp.maximum(best, s[:, j * 128:(j + 1) * 128])
            m = jnp.max(best, axis=1, keepdims=True)
            mc = jnp.where(m < 0.1 * LOW, 0.0, m) * SCALE2
            tot = jnp.zeros((128, 128), F32)
            out = jnp.zeros((128, 128), F32)
            for kc in range(nkeys // KEY_CHUNK):
                ks = slice(kc * KEY_CHUNK, (kc + 1) * KEY_CHUNK)
                pr = jnp.exp2(sc[hh, :, ks] * SCALE2 - mc)
                for j in range(KEY_CHUNK // 128):
                    tot = tot + pr[:, j * 128:(j + 1) * 128]
                out = out + dot(pr.astype(BF16), vals[hh, ks, :])
            total = jnp.sum(tot, axis=1, keepdims=True)
            stats = jnp.where(lane128 == 0, m * SCALE2, jnp.where(lane128 == 1, total, 0.0))
            st = stats.T[:8, :]
            ob = out.astype(BF16)
            head = p * 2 + hh
            o_send[head] = ob
            st_send[head] = st

            @pl.when(head != col)
            def _():
                for c in o_copy(head):
                    c.start()

            @pl.when(head == col)
            def _():
                o_recv[col] = ob
                st_recv[col] = st

        for at, acts in schedule.items():
            @pl.when(i == at)
            def _():
                for a in acts:
                    a()

    @pl.loop(1, ncol)
    def _(t):
        s = rem(col + t, ncol)
        pltpu.make_async_remote_copy(
            src_ref=o_send.at[s], dst_ref=o_recv.at[s], send_sem=o_ss.at[s], recv_sem=o_rs.at[s],
            device_id=(row, s), device_id_type=MESH).wait_recv()
        pltpu.make_async_remote_copy(
            src_ref=st_send.at[s], dst_ref=st_recv.at[s], send_sem=st_ss.at[s], recv_sem=st_rs.at[s],
            device_id=(row, s), device_id_type=MESH).wait_recv()

    ms, ls = st_recv[:, 0, :], st_recv[:, 1, :]
    top = jnp.max(ms, axis=0, keepdims=True)
    wgt = jnp.exp2(ms - top)
    share = wgt / jnp.sum(wgt * ls, axis=0, keepdims=True)
    share = jnp.concatenate([share, jnp.zeros((128 - ncol, 128), F32)], axis=0).T
    mix = jnp.zeros((128, 128), F32)
    for s in range(ncol):
        mix = mix + share[:, s:s + 1] * o_recv[s].astype(F32)
    mix = mix.astype(BF16)

    def slot_copy(send, recv, ss, rs, dest):
        return pltpu.make_async_remote_copy(
            src_ref=send.at[dest], dst_ref=recv.at[col], send_sem=ss.at[dest], recv_sem=rs.at[col],
            device_id=(row, dest), device_id_type=MESH)

    def arrive(send, recv, ss, rs):
        @pl.loop(1, ncol)
        def _(t):
            s = rem(col + t, ncol)
            pltpu.make_async_remote_copy(
                src_ref=send.at[s], dst_ref=recv.at[s], send_sem=ss.at[s], recv_sem=rs.at[s],
                device_id=(row, s), device_id_type=MESH).wait_recv()

    def spread(term, send, recv, ss, rs, dest):
        send[dest] = term

        @pl.when(dest != col)
        def _():
            slot_copy(send, recv, ss, rs, dest).start()

        @pl.when(dest == col)
        def _():
            recv[col] = term

    loads[2].wait()
    loads[3].wait()

    @pl.loop(0, pairs)
    def _(i):
        p = rem(first_pair + i, pairs)
        term = dot(mix, wo[:, pl.ds(pl.multiple_of(p * 256, 256), 256)]).astype(BF16)
        for hh in range(2):
            spread(term[:, hh * 128:(hh + 1) * 128], p1_send, p1_recv, p1_ss, p1_rs, p * 2 + hh)

    for t in range(2):
        stage_x(t, 1)
    arrive(p1_send, p1_recv, p1_ss, p1_rs)
    acc = hid[...].astype(F32)
    for s in range(ncol):
        acc = acc + p1_recv[s].astype(F32)
    att_mine = acc.astype(BF16)
    att[col] = att_mine

    def att_copy(dest):
        return pltpu.make_async_remote_copy(
            src_ref=att.at[col], dst_ref=att.at[col], send_sem=at_ss.at[dest], recv_sem=at_rs.at[col],
            device_id=(row, dest), device_id_type=MESH)

    @pl.loop(1, ncol)
    def _(t):
        att_copy(rem(col + t, ncol)).start()

    for t in range(2):
        stage_x2(t, 0)
    stage_x(2, 0)
    for t in range(2):
        stage_x2(t, 1)
    stage_y(2)

    @pl.loop(1, ncol)
    def _(t):
        s = rem(col + t, ncol)
        pltpu.make_async_remote_copy(
            src_ref=att.at[s], dst_ref=att.at[s], send_sem=at_ss.at[s], recv_sem=at_rs.at[s],
            device_id=(row, s), device_id_type=MESH).wait_recv()

    att_outs = [pltpu.make_async_copy(att.at[s], att_o.at[:, s * 128:(s + 1) * 128], out_sem.at[s])
                for s in range(ncol)]
    for c in att_outs:
        c.start()

    for c in own_loads:
        c.wait()
    sq = jnp.zeros((128, 128), F32)
    for s in range(ncol):
        a = att[s].astype(F32)
        sq = sq + a * a
    scale = lax.rsqrt(jnp.sum(sq, axis=1, keepdims=True) * (1.0 / (128 * ncol)) + 1e-06)
    for t in range(2):
        stage_sib(t)
    ff = gv.shape[2]
    gate = jnp.zeros((128, ff), F32)
    up = jnp.zeros((128, ff), F32)
    for s in range(0, ncol, 2):
        a = jnp.concatenate([att[s], att[s + 1]], axis=1).astype(F32)
        n = (a * scale).astype(BF16)
        gate = gate + dot(n, gv[s:s + 2].reshape(256, ff))
        up = up + dot(n, uv[s:s + 2].reshape(256, ff))
    act[...] = (gate / (1.0 + jnp.exp(-gate)) * up).astype(BF16)

    stage_x(2, 1)
    stage_x2(2, 0)
    stage_x2(2, 1)
    stage_sib(2)

    @pl.loop(0, pairs)
    def _(i):
        p = rem(first_pair + i, pairs)
        w = jnp.concatenate([dv[2 * p], dv[2 * p + 1]], axis=1)
        term = dot(act[...], w).astype(BF16)
        for hh in range(2):
            spread(term[:, hh * 128:(hh + 1) * 128], p2_send, p2_recv, p2_ss, p2_rs, p * 2 + hh)

    arrive(p2_send, p2_recv, p2_ss, p2_rs)
    acc = att[col].astype(F32)
    for s in range(ncol):
        acc = acc + p2_recv[s].astype(F32)
    blk[...] = acc.astype(BF16)
    blk_out = pltpu.make_async_copy(blk, blk_o, out_sem.at[ncol])
    blk_out.start()

    for t, owner, kind, dest, source in sent:
        wcopy(t, owner, kind, dest, source).wait_send()

    @pl.loop(1, ncol)
    def _(t):
        d = rem(col + t, ncol)
        for c in o_copy(d):
            c.wait_send()
        slot_copy(p1_send, p1_recv, p1_ss, p1_rs, d).wait_send()
        slot_copy(p2_send, p2_recv, p2_ss, p2_rs, d).wait_send()
        att_copy(d).wait_send()

    for c in att_outs:
        c.wait()
    blk_out.wait()


def solution(mesh):
    ncol, nrow = mesh.shape["col"], mesh.shape["row"]
    nx = nrow // 4
    placed = (
        P("row", None), P("col", None, None), P("col"), P("col"), P(), P("row", None), P(),
        P("col", None), P("row", "col"), P("row", "col"), P("col", "row"),
    )

    def on_device(queries, pool, table, plen, off, hidden, lup, wo, gate, up, down):
        rows, d = hidden.shape
        ff = gate.shape[1]
        nkeys = pool.shape[0] * pool.shape[1]
        dma, vm = pltpu.SemaphoreType.DMA, pltpu.VMEM
        anyspec = pl.BlockSpec(memory_space=pl.ANY)
        smem = pl.BlockSpec(memory_space=pltpu.SMEM)
        blocks = (ncol, rows, 128)
        scratch = [
            vm(pool.shape, BF16), vm((H // 2, LATENT, 512), BF16), vm(queries.shape, BF16),
            vm((rows, 128), BF16), vm(wo.shape, BF16),
            vm((nrow,) + gate.shape, BF16), vm((nrow,) + up.shape, BF16), vm((nrow,) + down.shape, BF16),
            vm((2, nkeys, 256), BF16), vm((2, nkeys, VDIM), BF16), vm((2, rows, nkeys), F32),
            vm((1, nkeys), jnp.int32),
            vm(blocks, BF16), vm(blocks, BF16), vm((ncol, 8, 128), F32), vm((ncol, 8, 128), F32),
            vm(blocks, BF16), vm(blocks, BF16), vm(blocks, BF16), vm(blocks, BF16), vm(blocks, BF16),
            vm((rows, ff), BF16), vm((rows, 128), BF16),
            dma((4,)), dma((H // 2,)), dma((3,)), dma((ncol + 1,)), dma((3, 5, nrow)), dma((3, nrow)),
        ] + [dma((ncol,))] * 10
        return pl.pallas_call(
            functools.partial(kernel, ncol, nx),
            out_shape=(
                jax.ShapeDtypeStruct((rows, d), BF16),
                jax.ShapeDtypeStruct((rows, d // ncol), BF16),
            ),
            in_specs=[anyspec, anyspec, smem, smem, smem] + [anyspec] * 6,
            out_specs=(anyspec, anyspec),
            scratch_shapes=scratch,
            compiler_params=pltpu.CompilerParams(
                collective_id=0, has_side_effects=True, vmem_limit_bytes=60 << 20),
            name="block",
        )(queries, pool, table, plen, off, hidden, lup, wo, gate, up, down)

    return jax.shard_map(
        on_device, mesh=mesh, in_specs=placed,
        out_specs=(P("row", None), P("row", "col")), check_vma=False,
    )
```

time: 875 us -> 101 us (0.12); the launches traced: 861 us -> 99.9 us
  waiting for transfers between devices: 523 us -> 0 us
  matrix products: 105 us -> 0 us
  Pallas kernels: 0 us -> 91.9 us
  blocking collectives: 76 us -> 0 us
  other arithmetic: 59.6 us -> 0 us
  loops' own time: 42.2 us -> 0 us
  local copies, waits for them, and re-layouts: 38.9 us -> 6.72 us
  between operations: 16.2 us -> 1.29 us
    all_gather x4 -> x0, waiting for transfers between devices: 314 us -> none  [the longest x1 283 us: joined(): everything = jax.tree.map(lambda part: lax.all_gather(part, axis), x)]
    psum x1 -> x0, waiting for transfers between devices: 147 us -> none  [on_device(): projected = lax.psum(partial_value, 'col')]
    dot_general x51 -> x0, matrix products: 105 us -> none  [the longest x16 39.3 us: one_head(): jnp.dot(latent_part, columns, preferred_element_type=jnp.float32)]
    pallas_call x0 -> x1, Pallas kernels: none -> 91.9 us  [on_device(): pl.pallas_call(functools.partial(kernel, ncol, nx), out_shape=(jax.ShapeD...]
    all_gather x2 -> x0, blocking collectives: 76 us -> none  [joined(): everything = jax.tree.map(lambda part: lax.all_gather(part, axis), x)]
    reduce_scatter x1 -> x0, waiting for transfers between devices: 60.2 us -> none  [on_device(): lax.psum_scatter(mlp_terms, 'col', scatter_dimension=1, tiled=True)]
    add x32 -> x0, other arithmetic: 47.3 us -> none  [the longest x15 47.1 us: join_partials(): left_weight[..., None] * left_out + right_weight[..., None] * right_out]
    another operation x2 -> x0, loops' own time: 42.2 us -> none  [the longest x1 42.2 us: on_device(): lax.map(one_head, jnp.arange(H, dtype=jnp.int32))]
  transfers between devices with their start and end apart: 6 -> 0, of which waited for: 4 -> 0; matrix products, arithmetic and copies ran while one was open for 1% -> 0% of each run, Pallas kernels for 0% -> 0%
where the time goes in v1:
time: 101 us; the launch traced here: 99.9 us
  Pallas kernels  91.9 us (91%)
  local copies, waits for them, and re-layouts  6.72 us (7%)
  between operations  1.29 us (1%)
    pallas_call x1, Pallas kernels, on_device(): pl.pallas_call(functools.partial(kernel, ncol, nx), out_shape=(jax.ShapeD...  91.9 us
    unnamed x4, local copies, waits for them, and re-layouts  6.72 us

profile of v1, /device:TPU:1, one launch (start us, length us, event | category | flops | bytes accessed | tf_op | source)
XLA Modules:
  0.0 99.9 jit_solution(10056691600675931273)
XLA Ops:
  1.3 1.7 %copy.13.g_h = bf16[128,684]{1,0:T(8,128)(2,1)} copy(bf16[128,684]{0,1:T(8,128)(2,1)} %param.19) | data formatting | bytes 350208 | tf_op args[8]
  3.0 1.7 %copy.14.u_h = bf16[128,684]{1,0:T(8,128)(2,1)} copy(bf16[128,684]{0,1:T(8,128)(2,1)} %param.20) | data formatting | bytes 350208 | tf_op args[9]
  4.7 91.9 %block.1 = (bf16[128,2048]{1,0:T(8,128)(2,1)}, bf16[128,128]{1,0:T(8,128)(2,1)}) custom-call(bf16[128,3072]{1,0:T(8,128)(2,1)} %q_h.1, bf16[32,64,576]{2,1,0:T(8,128)(2,1)} %pool_h.1, s32[32]{0:T(128)} %table_s.1, s32[32]{0:T(128)} %plen_s.1, s32[1]{0:T(128)S(6)} %copy.17.off_s, bf16[128,2048]{1,0:T(8,128)(2,1)} %hid_h.1, bf16[512,4096]{1,0:T(8,128)(2,1)} %lup_h.1, ...), custom_call_target="tpu_custom_call" | custom-call | tf_op jit(solution)/shard_map/block/pallas_call | solution.py:424
  96.7 1.9 %copy.18 = bf16[128,2048]{1,0:T(8,128)(2,1)} copy(bf16[128,2048]{1,0:T(8,128)(2,1)} %get-tuple-element.4) | data formatting | bytes 1048576
  98.5 1.4 %copy.19 = bf16[128,128]{1,0:T(8,128)(2,1)} copy(bf16[128,128]{1,0:T(8,128)(2,1)} %get-tuple-element.5) | data formatting | bytes 65536

commit v2 on v1

v2 whole, which is shorter than its diff:
```python
import functools
import math

import jax
import jax.numpy as jnp
from jax import lax
from jax.experimental import pallas as pl
from jax.experimental.pallas import tpu as pltpu
from jax.sharding import PartitionSpec as P

H = 16
NOPE = 128
ROPE = 64
VDIM = 128
LATENT = 512
QK = 192
MESH = pl.DeviceIdType.MESH
LOW = -1e30
FAR = 1 << 30
SCALE2 = math.log2(math.e) / math.sqrt(QK)
F32 = jnp.float32
BF16 = jnp.bfloat16
YP, XP, XM, SIB, DN = range(5)
KEY_CHUNK = 256
EXPAND = 512
EARLY, LATE = (0,), (0, 3, 6)
FAR_FIRST = (4, 3, 5, 2, 6, 1, 7)
NEAR_FIRST = (1, 7, 2, 6, 3, 5, 4)


def dot(a, b):
    return jnp.dot(a, b, preferred_element_type=F32)


def dot_nt(a, b):
    return lax.dot_general(a, b, (((1,), (1,)), ((), ())), preferred_element_type=F32)


def kernel(
    ncol, nx,
    q_h, pool_h, table_s, plen_s, off_s, hid_h, lup_h, wo_h, g_h, u_h, d_h,
    att_o, blk_o,
    lat, lupv, q2, hid, wo, gv, uv, dv, keys0, keys1, vals0, vals1, sc0, sc1, kpos,
    o_send, o_recv, st_send, st_recv, own_term, y1_send, y1_recv, z1_send, z1_recv, att,
    y2_send, y2_recv, z2_send, z2_recv, act, blk,
    lsem, lup_sem, q_sem, own_sem, out_sem, ws_sem, wr_sem, qs_sem, qr_sem,
    o_ss, o_rs, st_ss, st_rs, y1_ss, y1_rs, z1_ss, z1_rs, at_ss, at_rs, y2_ss, y2_rs, z2_ss, z2_rs,
):
    row, col = lax.axis_index("row"), lax.axis_index("col")

    def rem(a, b):
        return a % b

    def div(a, b):
        return a // b

    core, x, yhi = rem(row, 2), rem(div(row, 2), nx), div(row, 2 * nx)

    def row_of(yy, xx, cc):
        return (yy * nx + xx) * 2 + cc

    xp, xm, x2 = rem(x + 1, nx), rem(x + nx - 1, nx), rem(x + 2, nx)
    yo, co = 1 - yhi, 1 - core
    plus = [xp, xm, jnp.where(core == 0, xp, xm)]
    minus = [xm, xp, jnp.where(core == 0, xm, xp)]
    peers = [row_of(yo, x, core), row_of(yhi, xp, core), row_of(yhi, xm, core), row_of(yhi, x, co)]
    ups = [[row_of(yy, minus[t], core) for t in range(3)] for yy in (yhi, yo)]
    dns = [[row_of(yy, plus[t], core) for t in range(3)] for yy in (yhi, yo)]
    x2s = [row_of(yy, x2, core) for yy in (yhi, yo)]
    full = [gv, uv, dv]
    mine_h = [g_h, u_h, d_h]

    nz = ncol // 2
    z, ylo = div(col, 2), rem(col, 2)
    ynb = z * 2 + 1 - ylo
    sib = peers[SIB]
    steps = nz // 2
    turn = rem(core + z, 2)
    pair_at = [rem(z + 2 + 2 * i + turn, nz) for i in range(steps)]
    other_at = [rem(z + 2 + 2 * i + 1 - turn, nz) for i in range(steps)]

    loads = [
        pltpu.make_async_copy(pool_h, lat, lsem.at[0]),
        pltpu.make_async_copy(wo_h, wo, lsem.at[1]),
        pltpu.make_async_copy(hid_h.at[:, pl.ds(pl.multiple_of(col * 128, 128), 128)], hid, lsem.at[2]),
    ]

    def q_cols(p):
        return q_h.at[:, pl.ds(pl.multiple_of(p * 2 * QK, 2 * QK), 2 * QK)]

    lup_loads = [
        pltpu.make_async_copy(
            lup_h.at[:, pl.ds(pl.multiple_of(pair_at[i] * 512, 512), 512)], lupv.at[i], lup_sem.at[i])
        for i in range(steps)
    ]
    q_loads = [
        pltpu.make_async_copy(q_cols(pair_at[i]), q2.at[i, pl.ds(0, 128), :], q_sem.at[i])
        for i in range(steps)
    ]
    q_sends = [
        pltpu.make_async_remote_copy(
            src_ref=q_cols(other_at[i]), dst_ref=q2.at[i, pl.ds(128, 128), :],
            send_sem=qs_sem.at[i], recv_sem=qr_sem.at[i], device_id=(sib, col), device_id_type=MESH)
        for i in range(steps)
    ]
    lup_loads[0].start()
    loads[0].start()

    barrier = pltpu.get_barrier_semaphore()

    @pl.loop(1, ncol)
    def _(t):
        pl.semaphore_signal(barrier, inc=1, device_id=(row, rem(col + t, ncol)), device_id_type=MESH)

    @pl.loop(0, ncol)
    def _(t):
        pl.semaphore_signal(barrier, inc=1, device_id=(sib, rem(col + t, ncol)), device_id_type=MESH)

    for peer in peers[:SIB]:
        pl.semaphore_signal(barrier, inc=1, device_id=(peer, col), device_id_type=MESH)

    for c in q_loads + lup_loads[1:]:
        c.start()
    own_loads = [pltpu.make_async_copy(mine_h[t], full[t].at[row], own_sem.at[t]) for t in range(3)]
    for c in loads[1:] + own_loads:
        c.start()

    base = col * kpos.shape[1]
    lane = lax.broadcasted_iota(jnp.int32, kpos.shape, 1)
    page, slot = lax.shift_right_logical(lane, 6), lane & 63
    kp = jnp.full(kpos.shape, FAR, jnp.int32)
    for p in range(lat.shape[0]):
        here = jnp.where(slot < plen_s[p], base + p * 64 + slot, FAR)
        kp = jnp.where(page == table_s[p], here, kp)
    kpos[...] = kp
    sub = lax.broadcasted_iota(jnp.int32, (256, 1), 0)
    qpos = off_s[0] + jnp.where(sub < 128, row * 128 + sub, sib * 128 + sub - 128)

    nkeys = keys0.shape[1]
    bufs = [(keys0, vals0), (keys1, vals1)]

    def expand(i, kc, size):
        keys, vals = bufs[i % 2]
        rows = slice(kc * size, (kc + 1) * size)
        pages = slice(kc * size // 64, (kc + 1) * size // 64)
        e = dot(lat[pages, :, :LATENT].reshape(size, LATENT), lupv[i]).astype(BF16)
        keys[0, rows, :NOPE] = e[:, :128]
        vals[0, rows, :] = e[:, 128:256]
        keys[1, rows, :NOPE] = e[:, 256:384]
        vals[1, rows, :] = e[:, 384:]

    loads[0].wait()
    zeros64 = jnp.zeros((nkeys, 64), BF16)
    rope = jnp.concatenate([lat[:, :, LATENT:].reshape(nkeys, ROPE), zeros64], axis=1)
    for keys, _v in bufs:
        for hh in range(2):
            keys[hh, :, NOPE:] = rope
    lup_loads[0].wait()
    for kc in range(nkeys // EXPAND):
        expand(0, kc, EXPAND)

    pl.semaphore_wait(barrier, 2 * ncol - 1 + len(peers) - 1)
    for c in q_sends:
        c.start()

    sent = []

    def wcopy(t, owner, kind, dest, source=None):
        return pltpu.make_async_remote_copy(
            src_ref=full[t].at[owner] if source is None else source,
            dst_ref=full[t].at[owner],
            send_sem=ws_sem.at[t, kind, owner],
            recv_sem=wr_sem.at[t, owner],
            device_id=(dest, col),
            device_id_type=MESH,
        )

    def wsend(t, owner, kind, dest, source=None):
        wcopy(t, owner, kind, dest, source).start()
        sent.append((t, owner, kind, dest, source))

    def warrive(t, owner):
        wcopy(t, owner, SIB, sib).wait_recv()

    def stage_own(t):
        for kind in range(4):
            wsend(t, row, kind, peers[kind], mine_h[t])

    def stage_y(t):
        o = peers[YP]
        warrive(t, o)
        for kind in (XP, XM, SIB):
            wsend(t, o, kind, peers[kind])

    def stage_x(t, yy):
        up, dn = ups[yy][t], dns[yy][t]
        warrive(t, up)
        wsend(t, up, DN, dns[0][t])
        wsend(t, up, SIB, sib)
        warrive(t, dn)
        wsend(t, dn, SIB, sib)

    def stage_x2(t, yy):
        o = x2s[yy]
        warrive(t, o)
        wsend(t, o, SIB, sib)

    def stage_sib(t):
        for yy in range(2):
            for xx in range(nx):
                warrive(t, row_of(yy, xx, co))

    plan = {
        "start": [(stage_own, 0), (stage_own, 1)],
        1: [(stage_x, 0, 0), (stage_x, 1, 0), (stage_own, 2)],
        3: [(stage_y, 0), (stage_y, 1)],
        "proj_z": [(stage_x, 2, 0), (stage_y, 2)],
        "gather": [(stage_x, 0, 1), (stage_x, 1, 1), (stage_x2, 0, 0), (stage_x2, 1, 0)],
        "gather_y": [(stage_x2, 0, 1), (stage_x2, 1, 1), (stage_x, 2, 1), (stage_x2, 2, 0)],
        "gateup": [(stage_sib, 0), (stage_sib, 1)],
        "down": [(stage_x2, 2, 1), (stage_sib, 2)],
    }

    def at_point(name):
        for stage, *which in plan.get(name, ()):
            stage(*which)

    at_point("start")

    def o_copies(part, head):
        dest = sib if part else row
        return (
            pltpu.make_async_remote_copy(
                src_ref=o_send.at[part, head], dst_ref=o_recv.at[col], send_sem=o_ss.at[part, head],
                recv_sem=o_rs.at[col], device_id=(dest, head), device_id_type=MESH),
            pltpu.make_async_remote_copy(
                src_ref=st_send.at[part, head], dst_ref=st_recv.at[col], send_sem=st_ss.at[part, head],
                recv_sem=st_rs.at[col], device_id=(dest, head), device_id_type=MESH),
        )

    lane128 = lax.broadcasted_iota(jnp.int32, (128, 128), 1)
    scs = [sc0, sc1]
    nchunk = nkeys // KEY_CHUNK
    mine = rem(div(col, 2) + core, 2) == 0
    for i in range(steps):
        keys, vals = bufs[i % 2]
        more = i + 1 < steps
        q_loads[i].wait()
        q_sends[i].wait_recv()
        if more:
            lup_loads[i + 1].wait()
        zq = jnp.zeros((256, 64), BF16)
        qs = [jnp.concatenate([q2[i, :, hh * QK:(hh + 1) * QK], zq], axis=1) for hh in range(2)]
        best = [jnp.full((256, 128), LOW, F32)] * 2
        for kc in range(nchunk):
            ks = slice(kc * KEY_CHUNK, (kc + 1) * KEY_CHUNK)
            if more and kc in EARLY:
                expand(i + 1, EARLY.index(kc), EXPAND)
            for hh in range(2):
                s = dot_nt(qs[hh], keys[hh, ks, :])
                s = jnp.where(kpos[:, ks] <= qpos, s, LOW)
                scs[hh][:, ks] = s
                for j in range(KEY_CHUNK // 128):
                    best[hh] = jnp.maximum(best[hh], s[:, j * 128:(j + 1) * 128])
        ms = [jnp.max(b, axis=1, keepdims=True) for b in best]
        mc = [jnp.where(m < 0.1 * LOW, 0.0, m) * SCALE2 for m in ms]
        tot = [jnp.zeros((256, 128), F32)] * 2
        out = [jnp.zeros((256, 128), F32)] * 2
        for kc in range(nchunk):
            ks = slice(kc * KEY_CHUNK, (kc + 1) * KEY_CHUNK)
            if more and kc in LATE:
                expand(i + 1, len(EARLY) + LATE.index(kc), EXPAND)
            for hh in range(2):
                pr = jnp.exp2(scs[hh][:, ks] * SCALE2 - mc[hh])
                for j in range(KEY_CHUNK // 128):
                    tot[hh] = tot[hh] + pr[:, j * 128:(j + 1) * 128]
                out[hh] = out[hh] + dot(pr.astype(BF16), vals[hh, ks, :])
        for hh in range(2):
            head = pair_at[i] * 2 + hh
            total = jnp.sum(tot[hh], axis=1, keepdims=True)
            for part in range(2):
                rs = slice(part * 128, (part + 1) * 128)
                stats = jnp.where(lane128 == 0, ms[hh][rs] * SCALE2, jnp.where(lane128 == 1, total[rs], 0.0))
                o_send[part, head] = out[hh][rs].astype(BF16)
                st_send[part, head] = stats.T[:8, :]
        for hh in range(2):
            head = pair_at[i] * 2 + hh
            for c in o_copies(1, head):
                c.start()

            @pl.when(head != col)
            def _():
                for c in o_copies(0, head):
                    c.start()

            @pl.when(head == col)
            def _():
                o_recv[col] = o_send[0, col]
                st_recv[col] = st_send[0, col]

        at_point(i)

    def o_arrive(s):
        pltpu.make_async_remote_copy(
            src_ref=o_send.at[0, s], dst_ref=o_recv.at[s], send_sem=o_ss.at[0, s], recv_sem=o_rs.at[s],
            device_id=(sib, s), device_id_type=MESH).wait_recv()
        pltpu.make_async_remote_copy(
            src_ref=st_send.at[0, s], dst_ref=st_recv.at[s], send_sem=st_ss.at[0, s], recv_sem=st_rs.at[s],
            device_id=(sib, s), device_id_type=MESH).wait_recv()

    @pl.loop(1, ncol)
    def _(t):
        o_arrive(rem(col + t, ncol))

    @pl.when(jnp.logical_not(mine))
    def _():
        o_arrive(col)

    ms, ls = st_recv[:, 0, :], st_recv[:, 1, :]
    top = jnp.max(ms, axis=0, keepdims=True)
    wgt = jnp.exp2(ms - top)
    share = wgt / jnp.sum(wgt * ls, axis=0, keepdims=True)
    share = jnp.concatenate([share, jnp.zeros((128 - ncol, 128), F32)], axis=0).T
    mix = jnp.zeros((128, 128), F32)
    for s in range(ncol):
        mix = mix + share[:, s:s + 1] * o_recv[s].astype(F32)
    mix = mix.astype(BF16)

    def rcopy(src, dst, ss, rs, dest):
        return pltpu.make_async_remote_copy(
            src_ref=src, dst_ref=dst, send_sem=ss, recv_sem=rs, device_id=(row, dest), device_id_type=MESH)

    def y_copy(bufs5, zz):
        ys, yr, yss, yrs = bufs5[:4]
        return rcopy(ys.at[zz], yr.at[zz], yss.at[zz], yrs.at[zz], ynb)

    def z_copy(bufs5, zz, mine_slot):
        zs, zr, zss, zrs = bufs5[4:]
        return rcopy(zs.at[zz], zr.at[mine_slot], zss.at[zz], zrs.at[mine_slot], zz * 2 + ylo)

    def sum_over_col(term_of, start, bufs5, name):
        for off in FAR_FIRST + (0,):
            zz = rem(z + off, nz)
            both = term_of(zz)
            a, b = both[:, :128], both[:, 128:]
            own_term[zz] = jnp.where(ylo == 0, a, b)
            bufs5[0][zz] = jnp.where(ylo == 0, b, a).astype(BF16)
            y_copy(bufs5, zz).start()
        at_point(name + "_y")
        acc = start
        for off in FAR_FIRST + (0,):
            zz = rem(z + off, nz)
            y_copy(bufs5, zz).wait_recv()
            pair = own_term[zz] + bufs5[1][zz].astype(F32)
            if off:
                bufs5[4][zz] = pair.astype(BF16)
                z_copy(bufs5, zz, z).start()
            else:
                acc = acc + pair
        at_point(name + "_z")
        for off in NEAR_FIRST:
            zz = rem(z + off, nz)
            z_copy(bufs5, zz, zz).wait_recv()
            acc = acc + bufs5[5][zz].astype(F32)
        return acc

    set1 = (y1_send, y1_recv, y1_ss, y1_rs, z1_send, z1_recv, z1_ss, z1_rs)
    set2 = (y2_send, y2_recv, y2_ss, y2_rs, z2_send, z2_recv, z2_ss, z2_rs)

    loads[1].wait()
    loads[2].wait()
    att_mine = sum_over_col(
        lambda zz: dot(mix, wo[:, pl.ds(pl.multiple_of(zz * 256, 256), 256)]),
        hid[...].astype(F32), set1, "proj").astype(BF16)
    att[col] = att_mine

    def a_copy(slot, sem, dest):
        return rcopy(att.at[slot], att.at[slot], at_ss.at[sem], at_rs.at[slot], dest)

    a_sends = [(col, off, rem(z + off, nz) * 2 + ylo) for off in FAR_FIRST] + [(col, 0, ynb)]
    for a in a_sends:
        a_copy(*a).start()
    at_point("gather")
    for off in NEAR_FIRST:
        slot_z = rem(z + off, nz) * 2 + ylo
        a_copy(slot_z, 0, ynb).wait_recv()
        a_sends.append((slot_z, nz + off, ynb))
        a_copy(*a_sends[-1]).start()
    at_point("gather_y")
    for off in (0,) + NEAR_FIRST:
        a_copy(rem(z + off, nz) * 2 + 1 - ylo, 0, ynb).wait_recv()

    att_outs = [pltpu.make_async_copy(att.at[s], att_o.at[:, s * 128:(s + 1) * 128], out_sem.at[s])
                for s in range(ncol)]
    for c in att_outs:
        c.start()

    for c in own_loads:
        c.wait()
    sq = jnp.zeros((128, 128), F32)
    for s in range(ncol):
        a = att[s].astype(F32)
        sq = sq + a * a
    scale = lax.rsqrt(jnp.sum(sq, axis=1, keepdims=True) * (1.0 / (128 * ncol)) + 1e-06)
    at_point("gateup")
    ff = gv.shape[1]
    gate = jnp.zeros((128, ff), F32)
    up = jnp.zeros((128, ff), F32)
    for s in range(0, ncol, 2):
        a = jnp.concatenate([att[s], att[s + 1]], axis=1).astype(F32)
        n = (a * scale).astype(BF16)
        gate = gate + dot_nt(n, jnp.concatenate([gv[s], gv[s + 1]], axis=1))
        up = up + dot_nt(n, jnp.concatenate([uv[s], uv[s + 1]], axis=1))
    act[...] = (gate / (1.0 + jnp.exp(-gate)) * up).astype(BF16)

    at_point("down")
    blk[...] = sum_over_col(
        lambda zz: dot(act[...], jnp.concatenate([dv[zz * 2], dv[zz * 2 + 1]], axis=1)),
        att_mine.astype(F32), set2, "down").astype(BF16)
    blk_out = pltpu.make_async_copy(blk, blk_o, out_sem.at[ncol])
    blk_out.start()

    for t, owner, kind, dest, source in sent:
        wcopy(t, owner, kind, dest, source).wait_send()
    for i in range(steps):
        q_sends[i].wait_send()
        for hh in range(2):
            head = pair_at[i] * 2 + hh
            for c in o_copies(1, head):
                c.wait_send()

            @pl.when(head != col)
            def _():
                for c in o_copies(0, head):
                    c.wait_send()

    for bufs5 in (set1, set2):
        for off in range(nz):
            zz = rem(z + off, nz)
            y_copy(bufs5, zz).wait_send()
            if off:
                z_copy(bufs5, zz, z).wait_send()
    for a in a_sends:
        a_copy(*a).wait_send()
    for c in att_outs:
        c.wait()
    blk_out.wait()


def solution(mesh):
    ncol, nrow = mesh.shape["col"], mesh.shape["row"]
    nx = nrow // 4
    placed = (
        P("row", None), P("col", None, None), P("col"), P("col"), P(), P("row", None), P(),
        P("col", None), P("row", "col"), P("row", "col"), P("col", "row"),
    )

    def on_device(queries, pool, table, plen, off, hidden, lup, wo, gate, up, down):
        rows, d = hidden.shape
        gate, up = gate.T, up.T
        ff = gate.shape[0]
        nkeys = pool.shape[0] * pool.shape[1]
        dma, vm = pltpu.SemaphoreType.DMA, pltpu.VMEM
        anyspec = pl.BlockSpec(memory_space=pl.ANY)
        smem = pl.BlockSpec(memory_space=pltpu.SMEM)
        blocks, half = (ncol, rows, 128), (ncol // 2, rows, 128)
        steps = H // 4
        two = 2 * rows
        scratch = [
            vm(pool.shape, BF16), vm((steps, LATENT, 512), BF16), vm((steps, two, 2 * QK), BF16),
            vm((rows, 128), BF16), vm(wo.shape, BF16),
            vm((nrow,) + gate.shape, BF16), vm((nrow,) + up.shape, BF16), vm((nrow,) + down.shape, BF16),
            vm((2, nkeys, 256), BF16), vm((2, nkeys, 256), BF16),
            vm((2, nkeys, VDIM), BF16), vm((2, nkeys, VDIM), BF16),
            vm((two, nkeys), F32), vm((two, nkeys), F32), vm((1, nkeys), jnp.int32),
            vm((2,) + blocks, BF16), vm(blocks, BF16), vm((2, ncol, 8, 128), F32), vm((ncol, 8, 128), F32),
            vm(half, F32), vm(half, BF16), vm(half, BF16), vm(half, BF16), vm(half, BF16),
            vm(blocks, BF16), vm(half, BF16), vm(half, BF16), vm(half, BF16), vm(half, BF16),
            vm((rows, ff), BF16), vm((rows, 128), BF16),
            dma((3,)), dma((steps,)), dma((steps,)), dma((3,)), dma((ncol + 1,)), dma((3, 5, nrow)),
            dma((3, nrow)), dma((steps,)), dma((steps,)),
            dma((2, ncol)), dma((ncol,)), dma((2, ncol)), dma((ncol,)),
        ] + [dma((ncol // 2,))] * 4 + [dma((ncol,))] * 2 + [dma((ncol // 2,))] * 4
        return pl.pallas_call(
            functools.partial(kernel, ncol, nx),
            out_shape=(
                jax.ShapeDtypeStruct((rows, d), BF16),
                jax.ShapeDtypeStruct((rows, d // ncol), BF16),
            ),
            in_specs=[anyspec, anyspec, smem, smem, smem] + [anyspec] * 6,
            out_specs=(anyspec, anyspec),
            scratch_shapes=scratch,
            compiler_params=pltpu.CompilerParams(
                collective_id=0, has_side_effects=True, vmem_limit_bytes=60 << 20),
            name="block",
        )(queries, pool, table, plen, off, hidden, lup, wo, gate, up, down)

    return jax.shard_map(
        on_device, mesh=mesh, in_specs=placed,
        out_specs=(P("row", None), P("row", "col")), check_vma=False,
    )
```

time: 101 us -> 82.8 us (0.82)
  Pallas kernels: 91.9 us -> 78 us
  local copies, waits for them, and re-layouts: 6.72 us -> 3.26 us
    pallas_call x1, Pallas kernels: 91.9 us -> 78 us  [on_device(): pl.pallas_call(functools.partial(kernel, ncol, nx), out_shape=(jax.ShapeD...]
    unnamed x4 -> x2, local copies, waits for them, and re-layouts: 6.72 us -> 3.26 us
where the time goes in v2:
time: 82.8 us; the launch traced here: 82.6 us
  Pallas kernels  78 us (94%)
  local copies, waits for them, and re-layouts  3.26 us (4%)
  between operations  1.29 us (2%)
    pallas_call x1, Pallas kernels, on_device(): pl.pallas_call(functools.partial(kernel, ncol, nx), out_shape=(jax.ShapeD...  78 us
    unnamed x2, local copies, waits for them, and re-layouts  3.26 us

profile of v2, /device:TPU:1, one launch (start us, length us, event | category | flops | bytes accessed | tf_op | source)
XLA Modules:
  0.0 82.6 jit_solution(12018815081737034653)
XLA Ops:
  1.3 78.0 %block.1 = (bf16[128,2048]{1,0:T(8,128)(2,1)}, bf16[128,128]{1,0:T(8,128)(2,1)}) custom-call(bf16[128,3072]{1,0:T(8,128)(2,1)} %q_h.1, bf16[32,64,576]{2,1,0:T(8,128)(2,1)} %pool_h.1, s32[32]{0:T(128)} %table_s.1, s32[32]{0:T(128)} %plen_s.1, s32[1]{0:T(128)S(6)} %copy.15.off_s, bf16[128,2048]{1,0:T(8,128)(2,1)} %hid_h.1, bf16[512,4096]{1,0:T(8,128)(2,1)} %lup_h.1, ...), custom_call_target="tpu_custom_call" | custom-call | tf_op jit(solution)/shard_map/block/pallas_call | solution.py:484
  79.3 1.9 %copy.16 = bf16[128,2048]{1,0:T(8,128)(2,1)} copy(bf16[128,2048]{1,0:T(8,128)(2,1)} %get-tuple-element.4) | data formatting | bytes 1048576
  81.2 1.4 %copy.17 = bf16[128,128]{1,0:T(8,128)(2,1)} copy(bf16[128,128]{1,0:T(8,128)(2,1)} %get-tuple-element.5) | data formatting | bytes 65536

commit v3 on v2

--- a/solution.py
+++ b/solution.py
@@ -23,7 +23,8 @@
 YP, XP, XM, SIB, DN = range(5)
 KEY_CHUNK = 256
 EXPAND = 512
-EARLY, LATE = (0,), (0, 3, 6)
+LAG = 3
+BEFORE = 3
 FAR_FIRST = (4, 3, 5, 2, 6, 1, 7)
 NEAR_FIRST = (1, 7, 2, 6, 3, 5, 4)
 
@@ -40,10 +41,10 @@
     ncol, nx,
     q_h, pool_h, table_s, plen_s, off_s, hid_h, lup_h, wo_h, g_h, u_h, d_h,
     att_o, blk_o,
-    lat, lupv, q2, hid, wo, gv, uv, dv, keys0, keys1, vals0, vals1, sc0, sc1, kpos,
+    lat, lupv, q2, hid, wo, gv, uv, dv, keys_all, vals_all, sc0, sc1, pr0, pr1, kpos,
     o_send, o_recv, st_send, st_recv, own_term, y1_send, y1_recv, z1_send, z1_recv, att,
     y2_send, y2_recv, z2_send, z2_recv, act, blk,
-    lsem, lup_sem, q_sem, own_sem, out_sem, ws_sem, wr_sem, qs_sem, qr_sem,
+    lsem, lup_sem, q_sem, own_sem, out_sem, ws_sem, wr_sem, wsib_sem, qs_sem, qr_sem,
     o_ss, o_rs, st_ss, st_rs, y1_ss, y1_rs, z1_ss, z1_rs, at_ss, at_rs, y2_ss, y2_rs, z2_ss, z2_rs,
 ):
     row, col = lax.axis_index("row"), lax.axis_index("col")
@@ -100,7 +101,7 @@
     q_sends = [
         pltpu.make_async_remote_copy(
             src_ref=q_cols(other_at[i]), dst_ref=q2.at[i, pl.ds(128, 128), :],
-            send_sem=qs_sem.at[i], recv_sem=qr_sem.at[i], device_id=(sib, col), device_id_type=MESH)
+            send_sem=qs_sem, recv_sem=qr_sem.at[i], device_id=(sib, col), device_id_type=MESH)
         for i in range(steps)
     ]
     lup_loads[0].start()
@@ -136,11 +137,11 @@
     sub = lax.broadcasted_iota(jnp.int32, (256, 1), 0)
     qpos = off_s[0] + jnp.where(sub < 128, row * 128 + sub, sib * 128 + sub - 128)
 
-    nkeys = keys0.shape[1]
-    bufs = [(keys0, vals0), (keys1, vals1)]
+    nkeys = keys_all.shape[2]
+    bufs = [(keys_all.at[i], vals_all.at[i]) for i in range(steps)]
 
     def expand(i, kc, size):
-        keys, vals = bufs[i % 2]
+        keys, vals = bufs[i]
         rows = slice(kc * size, (kc + 1) * size)
         pages = slice(kc * size // 64, (kc + 1) * size // 64)
         e = dot(lat[pages, :, :LATENT].reshape(size, LATENT), lupv[i]).astype(BF16)
@@ -155,32 +156,40 @@
     for keys, _v in bufs:
         for hh in range(2):
             keys[hh, :, NOPE:] = rope
-    lup_loads[0].wait()
-    for kc in range(nkeys // EXPAND):
-        expand(0, kc, EXPAND)
+
+    def expand_pairs(first, last):
+        for i in range(first, last):
+            lup_loads[i].wait()
+            for kc in range(nkeys // EXPAND):
+                expand(i, kc, EXPAND)
+
+    expand_pairs(0, BEFORE)
 
     pl.semaphore_wait(barrier, 2 * ncol - 1 + len(peers) - 1)
     for c in q_sends:
         c.start()
-
-    sent = []
 
     def wcopy(t, owner, kind, dest, source=None):
         return pltpu.make_async_remote_copy(
             src_ref=full[t].at[owner] if source is None else source,
             dst_ref=full[t].at[owner],
-            send_sem=ws_sem.at[t, kind, owner],
-            recv_sem=wr_sem.at[t, owner],
+            send_sem=ws_sem.at[t],
+            recv_sem=wsib_sem.at[t] if kind == SIB else wr_sem.at[t, owner],
             device_id=(dest, col),
             device_id_type=MESH,
         )
 
+    def wgroup(t, count):
+        group = full[t].at[pl.ds(0, count)]
+        return pltpu.make_async_remote_copy(
+            src_ref=group, dst_ref=group, send_sem=ws_sem.at[t], recv_sem=wsib_sem.at[t],
+            device_id=(sib, col), device_id_type=MESH)
+
     def wsend(t, owner, kind, dest, source=None):
         wcopy(t, owner, kind, dest, source).start()
-        sent.append((t, owner, kind, dest, source))
 
     def warrive(t, owner):
-        wcopy(t, owner, SIB, sib).wait_recv()
+        wcopy(t, owner, DN, sib).wait_recv()
 
     def stage_own(t):
         for kind in range(4):
@@ -206,19 +215,16 @@
         wsend(t, o, SIB, sib)
 
     def stage_sib(t):
-        for yy in range(2):
-            for xx in range(nx):
-                warrive(t, row_of(yy, xx, co))
+        wgroup(t, 2 * nx).wait_recv()
 
     plan = {
         "start": [(stage_own, 0), (stage_own, 1)],
         1: [(stage_x, 0, 0), (stage_x, 1, 0), (stage_own, 2)],
         3: [(stage_y, 0), (stage_y, 1)],
-        "proj_z": [(stage_x, 2, 0), (stage_y, 2)],
-        "gather": [(stage_x, 0, 1), (stage_x, 1, 1), (stage_x2, 0, 0), (stage_x2, 1, 0)],
-        "gather_y": [(stage_x2, 0, 1), (stage_x2, 1, 1), (stage_x, 2, 1), (stage_x2, 2, 0)],
-        "gateup": [(stage_sib, 0), (stage_sib, 1)],
-        "down": [(stage_x2, 2, 1), (stage_sib, 2)],
+        "proj_z": [(stage_x, 2, 0), (stage_y, 2), (stage_x, 0, 1), (stage_x, 1, 1)],
+        "gather": [(stage_x2, 0, 0), (stage_x2, 1, 0), (stage_x2, 0, 1), (stage_x2, 1, 1),
+                   (stage_x, 2, 1), (stage_sib, 0), (stage_sib, 1)],
+        "down": [(stage_x2, 2, 0), (stage_x2, 2, 1), (stage_sib, 2)],
     }
 
     def at_point(name):
@@ -226,36 +232,32 @@
             stage(*which)
 
     at_point("start")
+    expand_pairs(BEFORE, steps)
 
     def o_copies(part, head):
         dest = sib if part else row
         return (
             pltpu.make_async_remote_copy(
-                src_ref=o_send.at[part, head], dst_ref=o_recv.at[col], send_sem=o_ss.at[part, head],
-                recv_sem=o_rs.at[col], device_id=(dest, head), device_id_type=MESH),
+                src_ref=o_send.at[part, head], dst_ref=o_recv.at[col], send_sem=o_ss.at[part],
+                recv_sem=o_rs, device_id=(dest, head), device_id_type=MESH),
             pltpu.make_async_remote_copy(
-                src_ref=st_send.at[part, head], dst_ref=st_recv.at[col], send_sem=st_ss.at[part, head],
-                recv_sem=st_rs.at[col], device_id=(dest, head), device_id_type=MESH),
+                src_ref=st_send.at[part, head], dst_ref=st_recv.at[col], send_sem=st_ss.at[part],
+                recv_sem=st_rs, device_id=(dest, head), device_id_type=MESH),
         )
 
     lane128 = lax.broadcasted_iota(jnp.int32, (128, 128), 1)
-    scs = [sc0, sc1]
+    scs, prs = [sc0, sc1], [pr0, pr1]
     nchunk = nkeys // KEY_CHUNK
     mine = rem(div(col, 2) + core, 2) == 0
     for i in range(steps):
-        keys, vals = bufs[i % 2]
-        more = i + 1 < steps
+        keys, vals = bufs[i]
         q_loads[i].wait()
         q_sends[i].wait_recv()
-        if more:
-            lup_loads[i + 1].wait()
         zq = jnp.zeros((256, 64), BF16)
         qs = [jnp.concatenate([q2[i, :, hh * QK:(hh + 1) * QK], zq], axis=1) for hh in range(2)]
         best = [jnp.full((256, 128), LOW, F32)] * 2
         for kc in range(nchunk):
             ks = slice(kc * KEY_CHUNK, (kc + 1) * KEY_CHUNK)
-            if more and kc in EARLY:
-                expand(i + 1, EARLY.index(kc), EXPAND)
             for hh in range(2):
                 s = dot_nt(qs[hh], keys[hh, ks, :])
                 s = jnp.where(kpos[:, ks] <= qpos, s, LOW)
@@ -264,17 +266,15 @@
                     best[hh] = jnp.maximum(best[hh], s[:, j * 128:(j + 1) * 128])
         ms = [jnp.max(b, axis=1, keepdims=True) for b in best]
         mc = [jnp.where(m < 0.1 * LOW, 0.0, m) * SCALE2 for m in ms]
-        tot = [jnp.zeros((256, 128), F32)] * 2
-        out = [jnp.zeros((256, 128), F32)] * 2
-        for kc in range(nchunk):
-            ks = slice(kc * KEY_CHUNK, (kc + 1) * KEY_CHUNK)
-            if more and kc in LATE:
-                expand(i + 1, len(EARLY) + LATE.index(kc), EXPAND)
-            for hh in range(2):
+        tot, out = [jnp.zeros((256, 128), F32)] * 2, [None, None]
+        for hh in range(2):
+            for kc in range(nchunk):
+                ks = slice(kc * KEY_CHUNK, (kc + 1) * KEY_CHUNK)
                 pr = jnp.exp2(scs[hh][:, ks] * SCALE2 - mc[hh])
                 for j in range(KEY_CHUNK // 128):
                     tot[hh] = tot[hh] + pr[:, j * 128:(j + 1) * 128]
-                out[hh] = out[hh] + dot(pr.astype(BF16), vals[hh, ks, :])
+                prs[hh][:, ks] = pr.astype(BF16)
+            out[hh] = dot(prs[hh][...], vals[hh])
         for hh in range(2):
             head = pair_at[i] * 2 + hh
             total = jnp.sum(tot[hh], axis=1, keepdims=True)
@@ -300,21 +300,26 @@
 
         at_point(i)
 
-    def o_arrive(s):
-        pltpu.make_async_remote_copy(
-            src_ref=o_send.at[0, s], dst_ref=o_recv.at[s], send_sem=o_ss.at[0, s], recv_sem=o_rs.at[s],
-            device_id=(sib, s), device_id_type=MESH).wait_recv()
-        pltpu.make_async_remote_copy(
-            src_ref=st_send.at[0, s], dst_ref=st_recv.at[s], send_sem=st_ss.at[0, s], recv_sem=st_rs.at[s],
-            device_id=(sib, s), device_id_type=MESH).wait_recv()
-
-    @pl.loop(1, ncol)
-    def _(t):
-        o_arrive(rem(col + t, ncol))
+    def o_group(part, count):
+        o, st = o_recv.at[pl.ds(0, count)], st_recv.at[pl.ds(0, count)]
+        return (
+            pltpu.make_async_remote_copy(
+                src_ref=o, dst_ref=o, send_sem=o_ss.at[part], recv_sem=o_rs,
+                device_id=(sib, col), device_id_type=MESH),
+            pltpu.make_async_remote_copy(
+                src_ref=st, dst_ref=st, send_sem=st_ss.at[part], recv_sem=st_rs,
+                device_id=(sib, col), device_id_type=MESH),
+        )
+
+    @pl.when(mine)
+    def _():
+        for c in o_group(0, ncol - 1):
+            c.wait_recv()
 
     @pl.when(jnp.logical_not(mine))
     def _():
-        o_arrive(col)
+        for c in o_group(0, ncol):
+            c.wait_recv()
 
     ms, ls = st_recv[:, 0, :], st_recv[:, 1, :]
     top = jnp.max(ms, axis=0, keepdims=True)
@@ -332,11 +337,11 @@
 
     def y_copy(bufs5, zz):
         ys, yr, yss, yrs = bufs5[:4]
-        return rcopy(ys.at[zz], yr.at[zz], yss.at[zz], yrs.at[zz], ynb)
+        return rcopy(ys.at[zz], yr.at[zz], yss, yrs.at[zz], ynb)
 
     def z_copy(bufs5, zz, mine_slot):
         zs, zr, zss, zrs = bufs5[4:]
-        return rcopy(zs.at[zz], zr.at[mine_slot], zss.at[zz], zrs.at[mine_slot], zz * 2 + ylo)
+        return rcopy(zs.at[zz], zr.at[mine_slot], zss, zrs.at[mine_slot], zz * 2 + ylo)
 
     def sum_over_col(term_of, start, bufs5, name):
         for off in FAR_FIRST + (0,):
@@ -374,77 +379,96 @@
         hid[...].astype(F32), set1, "proj").astype(BF16)
     att[col] = att_mine
 
-    def a_copy(slot, sem, dest):
-        return rcopy(att.at[slot], att.at[slot], at_ss.at[sem], at_rs.at[slot], dest)
-
-    a_sends = [(col, off, rem(z + off, nz) * 2 + ylo) for off in FAR_FIRST] + [(col, 0, ynb)]
-    for a in a_sends:
-        a_copy(*a).start()
-    at_point("gather")
-    for off in NEAR_FIRST:
-        slot_z = rem(z + off, nz) * 2 + ylo
-        a_copy(slot_z, 0, ynb).wait_recv()
-        a_sends.append((slot_z, nz + off, ynb))
-        a_copy(*a_sends[-1]).start()
-    at_point("gather_y")
-    for off in (0,) + NEAR_FIRST:
-        a_copy(rem(z + off, nz) * 2 + 1 - ylo, 0, ynb).wait_recv()
-
-    att_outs = [pltpu.make_async_copy(att.at[s], att_o.at[:, s * 128:(s + 1) * 128], out_sem.at[s])
-                for s in range(ncol)]
-    for c in att_outs:
-        c.start()
-
+    def a_copy(slot, dest):
+        return rcopy(att.at[slot], att.at[slot], at_ss, at_rs.at[slot], dest)
+
+    for off in FAR_FIRST:
+        a_copy(col, rem(z + off, nz) * 2 + ylo).start()
+    a_copy(col, ynb).start()
     for c in own_loads:
         c.wait()
-    sq = jnp.zeros((128, 128), F32)
-    for s in range(ncol):
-        a = att[s].astype(F32)
-        sq = sq + a * a
-    scale = lax.rsqrt(jnp.sum(sq, axis=1, keepdims=True) * (1.0 / (128 * ncol)) + 1e-06)
-    at_point("gateup")
+    at_point("gather")
     ff = gv.shape[1]
     gate = jnp.zeros((128, ff), F32)
     up = jnp.zeros((128, ff), F32)
-    for s in range(0, ncol, 2):
-        a = jnp.concatenate([att[s], att[s + 1]], axis=1).astype(F32)
-        n = (a * scale).astype(BF16)
-        gate = gate + dot_nt(n, jnp.concatenate([gv[s], gv[s + 1]], axis=1))
-        up = up + dot_nt(n, jnp.concatenate([uv[s], uv[s + 1]], axis=1))
+    sq = jnp.zeros((128, 128), F32)
+    order = (0,) + NEAR_FIRST
+    for k in range(nz + LAG):
+        if 0 < k < nz:
+            slot = rem(z + order[k], nz) * 2 + ylo
+            a_copy(slot, ynb).wait_recv()
+            a_copy(slot, ynb).start()
+        if k >= LAG:
+            zz = rem(z + order[k - LAG], nz)
+            a_copy(zz * 2 + 1 - ylo, ynb).wait_recv()
+            pltpu.make_async_copy(
+                att.at[zz * 2], att_o.at[:, pl.ds(pl.multiple_of(zz * 256, 256), 128)], out_sem.at[0]).start()
+            pltpu.make_async_copy(
+                att.at[zz * 2 + 1], att_o.at[:, pl.ds(pl.multiple_of(zz * 256 + 128, 128), 128)],
+                out_sem.at[0]).start()
+            n = jnp.concatenate([att[zz * 2], att[zz * 2 + 1]], axis=1)
+            gate = gate + dot_nt(n, jnp.concatenate([gv[zz * 2], gv[zz * 2 + 1]], axis=1))
+            up = up + dot_nt(n, jnp.concatenate([uv[zz * 2], uv[zz * 2 + 1]], axis=1))
+            wide = n.astype(F32)
+            wide = wide * wide
+            sq = sq + wide[:, :128] + wide[:, 128:]
+    scale = lax.rsqrt(jnp.sum(sq, axis=1, keepdims=True) * (1.0 / (128 * ncol)) + 1e-06)
+    gate, up = gate * scale, up * scale
     act[...] = (gate / (1.0 + jnp.exp(-gate)) * up).astype(BF16)
 
     at_point("down")
     blk[...] = sum_over_col(
         lambda zz: dot(act[...], jnp.concatenate([dv[zz * 2], dv[zz * 2 + 1]], axis=1)),
         att_mine.astype(F32), set2, "down").astype(BF16)
-    blk_out = pltpu.make_async_copy(blk, blk_o, out_sem.at[ncol])
+    blk_out = pltpu.make_async_copy(blk, blk_o, out_sem.at[1])
     blk_out.start()
 
-    for t, owner, kind, dest, source in sent:
-        wcopy(t, owner, kind, dest, source).wait_send()
-    for i in range(steps):
-        q_sends[i].wait_send()
-        for hh in range(2):
-            head = pair_at[i] * 2 + hh
-            for c in o_copies(1, head):
-                c.wait_send()
-
-            @pl.when(head != col)
-            def _():
-                for c in o_copies(0, head):
-                    c.wait_send()
-
-    for bufs5 in (set1, set2):
-        for off in range(nz):
-            zz = rem(z + off, nz)
-            y_copy(bufs5, zz).wait_send()
-            if off:
-                z_copy(bufs5, zz, z).wait_send()
-    for a in a_sends:
-        a_copy(*a).wait_send()
-    for c in att_outs:
+    for t in range(3):
+        wgroup(t, 15).wait_send()
+    q_all = q2.at[:, pl.ds(128, 128), :]
+    pltpu.make_async_remote_copy(
+        src_ref=q_all, dst_ref=q_all, send_sem=qs_sem, recv_sem=qr_sem.at[0],
+        device_id=(sib, col), device_id_type=MESH).wait_send()
+    for c in o_group(1, 2 * steps):
+        c.wait_send()
+
+    @pl.when(mine)
+    def _():
+        for c in o_group(0, 2 * steps - 1):
+            c.wait_send()
+
+    @pl.when(jnp.logical_not(mine))
+    def _():
+        for c in o_group(0, 2 * steps):
+            c.wait_send()
+
+    for ys, _yr, yss, yrs, zs, _zr, zss, zrs in (set1, set2):
+        rcopy(ys, ys, yss, yrs.at[0], ynb).wait_send()
+        most = zs.at[pl.ds(0, nz - 1)]
+        rcopy(most, most, zss, zrs.at[0], ynb).wait_send()
+    most = att.at[pl.ds(0, ncol - 1)]
+    rcopy(most, most, at_ss, at_rs.at[0], ynb).wait_send()
+    pltpu.make_async_copy(att_o, att_o, out_sem.at[0]).wait()
+    blk_out.wait()
+
+
+def write_out(a_h, b_h, a_o, b_o, a_v, b_v, sem):
+    parts = 4
+    size = a_v.shape[0] // parts
+
+    def rows(ref, i):
+        return ref.at[pl.ds(i * size, size), :]
+
+    pieces = [(rows(a_h, i), rows(a_v, i), rows(a_o, i)) for i in range(parts)] + [(b_h, b_v, b_o)]
+    ins = [pltpu.make_async_copy(h, v, sem.at[0, i]) for i, (h, v, o) in enumerate(pieces)]
+    outs = [pltpu.make_async_copy(v, o, sem.at[1, i]) for i, (h, v, o) in enumerate(pieces)]
+    for c in ins:
+        c.start()
+    for c, o in zip(ins, outs):
         c.wait()
-    blk_out.wait()
+        o.start()
+    for o in outs:
+        o.wait()
 
 
 def solution(mesh):
@@ -470,18 +494,19 @@
             vm(pool.shape, BF16), vm((steps, LATENT, 512), BF16), vm((steps, two, 2 * QK), BF16),
             vm((rows, 128), BF16), vm(wo.shape, BF16),
             vm((nrow,) + gate.shape, BF16), vm((nrow,) + up.shape, BF16), vm((nrow,) + down.shape, BF16),
-            vm((2, nkeys, 256), BF16), vm((2, nkeys, 256), BF16),
-            vm((2, nkeys, VDIM), BF16), vm((2, nkeys, VDIM), BF16),
-            vm((two, nkeys), F32), vm((two, nkeys), F32), vm((1, nkeys), jnp.int32),
+            vm((steps, 2, nkeys, 256), BF16), vm((steps, 2, nkeys, VDIM), BF16),
+            vm((two, nkeys), F32), vm((two, nkeys), F32), vm((two, nkeys), BF16), vm((two, nkeys), BF16),
+            vm((1, nkeys), jnp.int32),
             vm((2,) + blocks, BF16), vm(blocks, BF16), vm((2, ncol, 8, 128), F32), vm((ncol, 8, 128), F32),
             vm(half, F32), vm(half, BF16), vm(half, BF16), vm(half, BF16), vm(half, BF16),
             vm(blocks, BF16), vm(half, BF16), vm(half, BF16), vm(half, BF16), vm(half, BF16),
             vm((rows, ff), BF16), vm((rows, 128), BF16),
-            dma((3,)), dma((steps,)), dma((steps,)), dma((3,)), dma((ncol + 1,)), dma((3, 5, nrow)),
-            dma((3, nrow)), dma((steps,)), dma((steps,)),
-            dma((2, ncol)), dma((ncol,)), dma((2, ncol)), dma((ncol,)),
-        ] + [dma((ncol // 2,))] * 4 + [dma((ncol,))] * 2 + [dma((ncol // 2,))] * 4
-        return pl.pallas_call(
+            dma((3,)), dma((steps,)), dma((steps,)), dma((3,)), dma((2,)), dma((3,)), dma((3, nrow)), dma((3,)),
+            dma, dma((steps,)), dma((2,)), dma, dma((2,)), dma,
+            dma, dma((ncol // 2,)), dma, dma((ncol // 2,)), dma, dma((ncol,)),
+            dma, dma((ncol // 2,)), dma, dma((ncol // 2,)),
+        ]
+        att, blk = pl.pallas_call(
             functools.partial(kernel, ncol, nx),
             out_shape=(
                 jax.ShapeDtypeStruct((rows, d), BF16),
@@ -494,6 +519,17 @@
                 collective_id=0, has_side_effects=True, vmem_limit_bytes=60 << 20),
             name="block",
         )(queries, pool, table, plen, off, hidden, lup, wo, gate, up, down)
+        return pl.pallas_call(
+            write_out,
+            out_shape=(
+                jax.ShapeDtypeStruct(att.shape, BF16),
+                jax.ShapeDtypeStruct(blk.shape, BF16),
+            ),
+            in_specs=[anyspec] * 2,
+            out_specs=(anyspec, anyspec),
+            scratch_shapes=[vm(att.shape, BF16), vm(blk.shape, BF16), dma((2, 5))],
+            name="write_out",
+        )(att, blk)
 
     return jax.shard_map(
         on_device, mesh=mesh, in_specs=placed,

time: 82.8 us -> 79 us (0.954)
  local copies, waits for them, and re-layouts: 3.26 us -> 0 us
    unnamed x2 -> x0, local copies, waits for them, and re-layouts: 3.26 us -> none
    pallas_call x1, Pallas kernels: 78 us -> 75.6 us  [on_device(): pl.pallas_call(functools.partial(kernel, ncol, nx), out_shape=(jax.ShapeD...]
    pallas_call x0 -> x1, Pallas kernels: none -> 1.84 us  [on_device(): pl.pallas_call(write_out, out_shape=(jax.ShapeDtypeStruct(att.shape, BF16...]
where the time goes in v3:
time: 79 us; the launch traced here: 78.9 us
  Pallas kernels  77.4 us (98%)
  between operations  1.45 us (2%)
    pallas_call x1, Pallas kernels, on_device(): pl.pallas_call(functools.partial(kernel, ncol, nx), out_shape=(jax.ShapeD...  75.6 us
    pallas_call x1, Pallas kernels, on_device(): pl.pallas_call(write_out, out_shape=(jax.ShapeDtypeStruct(att.shape, BF16...  1.84 us

profile of v3, /device:TPU:1, one launch (start us, length us, event | category | flops | bytes accessed | tf_op | source)
XLA Modules:
  0.0 78.9 jit_solution(5316419189120642606)
XLA Ops:
  1.3 75.6 %block.1 = (bf16[128,2048]{1,0:T(8,128)(2,1)}, bf16[128,128]{1,0:T(8,128)(2,1)}) custom-call(bf16[128,3072]{1,0:T(8,128)(2,1)} %q_h.1, bf16[32,64,576]{2,1,0:T(8,128)(2,1)} %pool_h.1, s32[32]{0:T(128)} %table_s.1, s32[32]{0:T(128)} %plen_s.1, s32[1]{0:T(128)S(6)} %copy.13.off_s, bf16[128,2048]{1,0:T(8,128)(2,1)} %hid_h.1, bf16[512,4096]{1,0:T(8,128)(2,1)} %lup_h.1, ...), custom_call_target="tpu_custom_call" | custom-call | tf_op jit(solution)/shard_map/block/pallas_call | solution.py:509
  76.9 1.8 %write_out.1 = (bf16[128,2048]{1,0:T(8,128)(2,1)}, bf16[128,128]{1,0:T(8,128)(2,1)}) custom-call(bf16[128,2048]{1,0:T(8,128)(2,1)} %get-tuple-element.4.a_h, bf16[128,128]{1,0:T(8,128)(2,1)} %get-tuple-element.5.b_h), custom_call_target="tpu_custom_call" | custom-call | tf_op jit(solution)/shard_map/write_out/pallas_call | solution.py:522

commit v4 on v3

--- a/solution.py
+++ b/solution.py
@@ -24,7 +24,7 @@
 KEY_CHUNK = 256
 EXPAND = 512
 LAG = 3
-BEFORE = 3
+ROWS = 16
 FAR_FIRST = (4, 3, 5, 2, 6, 1, 7)
 NEAR_FIRST = (1, 7, 2, 6, 3, 5, 4)
 
@@ -41,7 +41,7 @@
     ncol, nx,
     q_h, pool_h, table_s, plen_s, off_s, hid_h, lup_h, wo_h, g_h, u_h, d_h,
     att_o, blk_o,
-    lat, lupv, q2, hid, wo, gv, uv, dv, keys_all, vals_all, sc0, sc1, pr0, pr1, kpos,
+    lat, lupv, q2, hid, wo, gv, uv, dv, keys_all, vals_all, sc0, sc1, pr0, pr1, kpos, bias, bst, mx,
     o_send, o_recv, st_send, st_recv, own_term, y1_send, y1_recv, z1_send, z1_recv, att,
     y2_send, y2_recv, z2_send, z2_recv, act, blk,
     lsem, lup_sem, q_sem, own_sem, out_sem, ws_sem, wr_sem, wsib_sem, qs_sem, qr_sem,
@@ -138,6 +138,12 @@
     qpos = off_s[0] + jnp.where(sub < 128, row * 128 + sub, sib * 128 + sub - 128)
 
     nkeys = keys_all.shape[2]
+
+    def make_bias():
+        for rb in range(0, 256, 16):
+            seen = kpos[...] <= qpos[rb:rb + 16]
+            bias[rb:rb + 16, :] = jnp.where(seen, 0.0, LOW)
+
     bufs = [(keys_all.at[i], vals_all.at[i]) for i in range(steps)]
 
     def expand(i, kc, size):
@@ -150,21 +156,6 @@
         keys[1, rows, :NOPE] = e[:, 256:384]
         vals[1, rows, :] = e[:, 384:]
 
-    loads[0].wait()
-    zeros64 = jnp.zeros((nkeys, 64), BF16)
-    rope = jnp.concatenate([lat[:, :, LATENT:].reshape(nkeys, ROPE), zeros64], axis=1)
-    for keys, _v in bufs:
-        for hh in range(2):
-            keys[hh, :, NOPE:] = rope
-
-    def expand_pairs(first, last):
-        for i in range(first, last):
-            lup_loads[i].wait()
-            for kc in range(nkeys // EXPAND):
-                expand(i, kc, EXPAND)
-
-    expand_pairs(0, BEFORE)
-
     pl.semaphore_wait(barrier, 2 * ncol - 1 + len(peers) - 1)
     for c in q_sends:
         c.start()
@@ -219,11 +210,12 @@
 
     plan = {
         "start": [(stage_own, 0), (stage_own, 1)],
-        1: [(stage_x, 0, 0), (stage_x, 1, 0), (stage_own, 2)],
-        3: [(stage_y, 0), (stage_y, 1)],
-        "proj_z": [(stage_x, 2, 0), (stage_y, 2), (stage_x, 0, 1), (stage_x, 1, 1)],
-        "gather": [(stage_x2, 0, 0), (stage_x2, 1, 0), (stage_x2, 0, 1), (stage_x2, 1, 1),
-                   (stage_x, 2, 1), (stage_sib, 0), (stage_sib, 1)],
+        0: [(stage_x, 0, 0), (stage_x, 1, 0), (stage_own, 2)],
+        2: [(stage_y, 0), (stage_y, 1)],
+        3: [(stage_x, 2, 0)],
+        "proj_y": [(stage_y, 2), (stage_x, 0, 1), (stage_x, 1, 1)],
+        "proj_z": [(stage_x2, 0, 0), (stage_x2, 1, 0)],
+        "gather": [(stage_x2, 0, 1), (stage_x2, 1, 1), (stage_x, 2, 1), (stage_sib, 0), (stage_sib, 1)],
         "down": [(stage_x2, 2, 0), (stage_x2, 2, 1), (stage_sib, 2)],
     }
 
@@ -232,7 +224,22 @@
             stage(*which)
 
     at_point("start")
-    expand_pairs(BEFORE, steps)
+
+    loads[0].wait()
+    zeros64 = jnp.zeros((nkeys, 64), BF16)
+    rope = jnp.concatenate([lat[:, :, LATENT:].reshape(nkeys, ROPE), zeros64], axis=1)
+    for keys, _v in bufs:
+        for hh in range(2):
+            keys[hh, :, NOPE:] = rope
+
+
+    def expand_pairs(first, last):
+        for i in range(first, last):
+            lup_loads[i].wait()
+            for kc in range(nkeys // EXPAND):
+                expand(i, kc, EXPAND)
+
+    expand_pairs(0, steps)
 
     def o_copies(part, head):
         dest = sib if part else row
@@ -249,39 +256,51 @@
     scs, prs = [sc0, sc1], [pr0, pr1]
     nchunk = nkeys // KEY_CHUNK
     mine = rem(div(col, 2) + core, 2) == 0
+    make_bias()
     for i in range(steps):
-        keys, vals = bufs[i]
         q_loads[i].wait()
         q_sends[i].wait_recv()
-        zq = jnp.zeros((256, 64), BF16)
-        qs = [jnp.concatenate([q2[i, :, hh * QK:(hh + 1) * QK], zq], axis=1) for hh in range(2)]
-        best = [jnp.full((256, 128), LOW, F32)] * 2
-        for kc in range(nchunk):
-            ks = slice(kc * KEY_CHUNK, (kc + 1) * KEY_CHUNK)
-            for hh in range(2):
-                s = dot_nt(qs[hh], keys[hh, ks, :])
-                s = jnp.where(kpos[:, ks] <= qpos, s, LOW)
-                scs[hh][:, ks] = s
-                for j in range(KEY_CHUNK // 128):
-                    best[hh] = jnp.maximum(best[hh], s[:, j * 128:(j + 1) * 128])
-        ms = [jnp.max(b, axis=1, keepdims=True) for b in best]
-        mc = [jnp.where(m < 0.1 * LOW, 0.0, m) * SCALE2 for m in ms]
-        tot, out = [jnp.zeros((256, 128), F32)] * 2, [None, None]
+    zq = jnp.zeros((256, 64), BF16)
+    ones = jnp.ones((nkeys, 128), BF16)
+
+    def score(n, kc):
+        i, hh = n // 2, n % 2
+        q = jnp.concatenate([q2[i, :, hh * QK:(hh + 1) * QK], zq], axis=1)
+        ks = slice(kc * KEY_CHUNK, (kc + 1) * KEY_CHUNK)
+        t = dot_nt(q, bufs[i][0][hh, ks, :]) * SCALE2 + bias[:, ks]
+        scs[hh][:, ks] = t
+        best = t[:, :128]
+        for c in range(1, KEY_CHUNK // 128):
+            best = jnp.maximum(best, t[:, c * 128:(c + 1) * 128])
+        bst[hh] = best if kc == 0 else jnp.maximum(best, bst[hh])
+
+    def soft(hh, rb):
+        rows = slice(rb * ROWS, (rb + 1) * ROWS)
+        m = mx[hh, rows, :]
+        for c in range(nkeys // 128):
+            ks = slice(c * 128, (c + 1) * 128)
+            prs[hh][rows, ks] = jnp.exp2(scs[hh][rows, ks] - m).astype(BF16)
+
+    for kc in range(nchunk):
+        score(0, kc)
+    for i in range(steps):
         for hh in range(2):
+            n = 2 * i + hh
+            m = jnp.max(bst[hh], axis=1, keepdims=True)
+            mx[hh] = jnp.broadcast_to(jnp.where(m < 0.01 * LOW, 0.0, m), mx.shape[1:])
             for kc in range(nchunk):
-                ks = slice(kc * KEY_CHUNK, (kc + 1) * KEY_CHUNK)
-                pr = jnp.exp2(scs[hh][:, ks] * SCALE2 - mc[hh])
-                for j in range(KEY_CHUNK // 128):
-                    tot[hh] = tot[hh] + pr[:, j * 128:(j + 1) * 128]
-                prs[hh][:, ks] = pr.astype(BF16)
-            out[hh] = dot(prs[hh][...], vals[hh])
-        for hh in range(2):
+                for rb in range(256 // ROWS // nchunk):
+                    soft(hh, kc * (256 // ROWS // nchunk) + rb)
+                if n + 1 < 2 * steps:
+                    score(n + 1, kc)
+            out = dot(prs[hh][...], jnp.concatenate([bufs[i][1][hh], ones], axis=1))
             head = pair_at[i] * 2 + hh
-            total = jnp.sum(tot[hh], axis=1, keepdims=True)
             for part in range(2):
                 rs = slice(part * 128, (part + 1) * 128)
-                stats = jnp.where(lane128 == 0, ms[hh][rs] * SCALE2, jnp.where(lane128 == 1, total[rs], 0.0))
-                o_send[part, head] = out[hh][rs].astype(BF16)
+                total = out[rs, 128:]
+                top = jnp.where(total > 0.0, mx[hh, rs, :], LOW)
+                stats = jnp.where(lane128 == 0, top, jnp.where(lane128 == 1, total, 0.0))
+                o_send[part, head] = out[rs, :128].astype(BF16)
                 st_send[part, head] = stats.T[:8, :]
         for hh in range(2):
             head = pair_at[i] * 2 + hh
@@ -496,7 +515,8 @@
             vm((nrow,) + gate.shape, BF16), vm((nrow,) + up.shape, BF16), vm((nrow,) + down.shape, BF16),
             vm((steps, 2, nkeys, 256), BF16), vm((steps, 2, nkeys, VDIM), BF16),
             vm((two, nkeys), F32), vm((two, nkeys), F32), vm((two, nkeys), BF16), vm((two, nkeys), BF16),
-            vm((1, nkeys), jnp.int32),
+            vm((1, nkeys), jnp.int32), vm((two, nkeys), F32),
+            vm((2, two, 128), F32), vm((2, two, 128), F32),
             vm((2,) + blocks, BF16), vm(blocks, BF16), vm((2, ncol, 8, 128), F32), vm((ncol, 8, 128), F32),
             vm(half, F32), vm(half, BF16), vm(half, BF16), vm(half, BF16), vm(half, BF16),
             vm(blocks, BF16), vm(half, BF16), vm(half, BF16), vm(half, BF16), vm(half, BF16),

time: 79 us -> 82.4 us (1.043)
  Pallas kernels: 77.4 us -> 80.8 us
    pallas_call x1, Pallas kernels: 75.6 us -> 79 us  [on_device(): pl.pallas_call(functools.partial(kernel, ncol, nx), out_shape=(jax.ShapeD...]
where the time goes in v4:
time: 82.4 us; the launch traced here: 82.3 us
  Pallas kernels  80.8 us (98%)
  between operations  1.45 us (2%)
    pallas_call x1, Pallas kernels, on_device(): pl.pallas_call(functools.partial(kernel, ncol, nx), out_shape=(jax.ShapeD...  79 us
    pallas_call x1, Pallas kernels, on_device(): pl.pallas_call(write_out, out_shape=(jax.ShapeDtypeStruct(att.shape, BF16...  1.84 us

profile of v4, /device:TPU:1, one launch (start us, length us, event | category | flops | bytes accessed | tf_op | source)
XLA Modules:
  0.0 82.3 jit_solution(10849573184510599987)
XLA Ops:
  1.3 79.0 %block.1 = (bf16[128,2048]{1,0:T(8,128)(2,1)}, bf16[128,128]{1,0:T(8,128)(2,1)}) custom-call(bf16[128,3072]{1,0:T(8,128)(2,1)} %q_h.1, bf16[32,64,576]{2,1,0:T(8,128)(2,1)} %pool_h.1, s32[32]{0:T(128)} %table_s.1, s32[32]{0:T(128)} %plen_s.1, s32[1]{0:T(128)S(6)} %copy.13.off_s, bf16[128,2048]{1,0:T(8,128)(2,1)} %hid_h.1, bf16[512,4096]{1,0:T(8,128)(2,1)} %lup_h.1, ...), custom_call_target="tpu_custom_call" | custom-call | tf_op jit(solution)/shard_map/block/pallas_call | solution.py:529
  80.3 1.8 %write_out.1 = (bf16[128,2048]{1,0:T(8,128)(2,1)}, bf16[128,128]{1,0:T(8,128)(2,1)}) custom-call(bf16[128,2048]{1,0:T(8,128)(2,1)} %get-tuple-element.4.a_h, bf16[128,128]{1,0:T(8,128)(2,1)} %get-tuple-element.5.b_h), custom_call_target="tpu_custom_call" | custom-call | tf_op jit(solution)/shard_map/write_out/pallas_call | solution.py:542

commit v5 on v4

--- a/solution.py
+++ b/solution.py
@@ -25,6 +25,7 @@
 EXPAND = 512
 LAG = 3
 ROWS = 16
+BEFORE = 2
 FAR_FIRST = (4, 3, 5, 2, 6, 1, 7)
 NEAR_FIRST = (1, 7, 2, 6, 3, 5, 4)
 
@@ -156,6 +157,23 @@
         keys[1, rows, :NOPE] = e[:, 256:384]
         vals[1, rows, :] = e[:, 384:]
 
+    make_bias()
+    loads[0].wait()
+    zeros64 = jnp.zeros((nkeys, 64), BF16)
+    rope = jnp.concatenate([lat[:, :, LATENT:].reshape(nkeys, ROPE), zeros64], axis=1)
+    for keys, _v in bufs:
+        for hh in range(2):
+            keys[hh, :, NOPE:] = rope
+
+
+    def expand_pairs(first, last):
+        for i in range(first, last):
+            lup_loads[i].wait()
+            for kc in range(nkeys // EXPAND):
+                expand(i, kc, EXPAND)
+
+    expand_pairs(0, BEFORE)
+
     pl.semaphore_wait(barrier, 2 * ncol - 1 + len(peers) - 1)
     for c in q_sends:
         c.start()
@@ -209,13 +227,13 @@
         wgroup(t, 2 * nx).wait_recv()
 
     plan = {
-        "start": [(stage_own, 0), (stage_own, 1)],
-        0: [(stage_x, 0, 0), (stage_x, 1, 0), (stage_own, 2)],
-        2: [(stage_y, 0), (stage_y, 1)],
-        3: [(stage_x, 2, 0)],
-        "proj_y": [(stage_y, 2), (stage_x, 0, 1), (stage_x, 1, 1)],
-        "proj_z": [(stage_x2, 0, 0), (stage_x2, 1, 0)],
-        "gather": [(stage_x2, 0, 1), (stage_x2, 1, 1), (stage_x, 2, 1), (stage_sib, 0), (stage_sib, 1)],
+        "start": [(stage_own, 0), (stage_own, 1), (stage_own, 2)],
+        1: [(stage_x, 0, 0), (stage_x, 1, 0)],
+        3: [(stage_y, 0), (stage_y, 1), (stage_x, 2, 0)],
+        "proj_z": [(stage_y, 2)],
+        "gather": [(stage_x, 0, 1), (stage_x, 1, 1), (stage_x2, 0, 0), (stage_x2, 1, 0)],
+        "block0": [(stage_x2, 0, 1), (stage_x2, 1, 1), (stage_sib, 0), (stage_sib, 1)],
+        "block4": [(stage_x, 2, 1)],
         "down": [(stage_x2, 2, 0), (stage_x2, 2, 1), (stage_sib, 2)],
     }
 
@@ -225,21 +243,7 @@
 
     at_point("start")
 
-    loads[0].wait()
-    zeros64 = jnp.zeros((nkeys, 64), BF16)
-    rope = jnp.concatenate([lat[:, :, LATENT:].reshape(nkeys, ROPE), zeros64], axis=1)
-    for keys, _v in bufs:
-        for hh in range(2):
-            keys[hh, :, NOPE:] = rope
-
-
-    def expand_pairs(first, last):
-        for i in range(first, last):
-            lup_loads[i].wait()
-            for kc in range(nkeys // EXPAND):
-                expand(i, kc, EXPAND)
-
-    expand_pairs(0, steps)
+    expand_pairs(BEFORE, steps)
 
     def o_copies(part, head):
         dest = sib if part else row
@@ -256,7 +260,6 @@
     scs, prs = [sc0, sc1], [pr0, pr1]
     nchunk = nkeys // KEY_CHUNK
     mine = rem(div(col, 2) + core, 2) == 0
-    make_bias()
     for i in range(steps):
         q_loads[i].wait()
         q_sends[i].wait_recv()
@@ -418,6 +421,7 @@
             a_copy(slot, ynb).wait_recv()
             a_copy(slot, ynb).start()
         if k >= LAG:
+            at_point(f"block{k - LAG}")
             zz = rem(z + order[k - LAG], nz)
             a_copy(zz * 2 + 1 - ylo, ynb).wait_recv()
             pltpu.make_async_copy(

time: 82.4 us -> 79.3 us (0.962)
  Pallas kernels: 80.8 us -> 77.7 us
    pallas_call x1, Pallas kernels: 79 us -> 75.8 us  [on_device(): pl.pallas_call(functools.partial(kernel, ncol, nx), out_shape=(jax.ShapeD...]
where the time goes in v5:
time: 79.3 us; the launch traced here: 79.1 us
  Pallas kernels  77.7 us (98%)
  between operations  1.45 us (2%)
    pallas_call x1, Pallas kernels, on_device(): pl.pallas_call(functools.partial(kernel, ncol, nx), out_shape=(jax.ShapeD...  75.8 us
    pallas_call x1, Pallas kernels, on_device(): pl.pallas_call(write_out, out_shape=(jax.ShapeDtypeStruct(att.shape, BF16...  1.84 us

profile of v5, /device:TPU:1, one launch (start us, length us, event | category | flops | bytes accessed | tf_op | source)
XLA Modules:
  0.0 79.1 jit_solution(5082195778656563526)
XLA Ops:
  1.3 75.8 %block.1 = (bf16[128,2048]{1,0:T(8,128)(2,1)}, bf16[128,128]{1,0:T(8,128)(2,1)}) custom-call(bf16[128,3072]{1,0:T(8,128)(2,1)} %q_h.1, bf16[32,64,576]{2,1,0:T(8,128)(2,1)} %pool_h.1, s32[32]{0:T(128)} %table_s.1, s32[32]{0:T(128)} %plen_s.1, s32[1]{0:T(128)S(6)} %copy.13.off_s, bf16[128,2048]{1,0:T(8,128)(2,1)} %hid_h.1, bf16[512,4096]{1,0:T(8,128)(2,1)} %lup_h.1, ...), custom_call_target="tpu_custom_call" | custom-call | tf_op jit(solution)/shard_map/block/pallas_call | solution.py:533
  77.1 1.8 %write_out.1 = (bf16[128,2048]{1,0:T(8,128)(2,1)}, bf16[128,128]{1,0:T(8,128)(2,1)}) custom-call(bf16[128,2048]{1,0:T(8,128)(2,1)} %get-tuple-element.4.a_h, bf16[128,128]{1,0:T(8,128)(2,1)} %get-tuple-element.5.b_h), custom_call_target="tpu_custom_call" | custom-call | tf_op jit(solution)/shard_map/write_out/pallas_call | solution.py:546

commit v6 on v5

--- a/solution.py
+++ b/solution.py
@@ -228,12 +228,11 @@
 
     plan = {
         "start": [(stage_own, 0), (stage_own, 1), (stage_own, 2)],
-        1: [(stage_x, 0, 0), (stage_x, 1, 0)],
-        3: [(stage_y, 0), (stage_y, 1), (stage_x, 2, 0)],
-        "proj_z": [(stage_y, 2)],
-        "gather": [(stage_x, 0, 1), (stage_x, 1, 1), (stage_x2, 0, 0), (stage_x2, 1, 0)],
-        "block0": [(stage_x2, 0, 1), (stage_x2, 1, 1), (stage_sib, 0), (stage_sib, 1)],
-        "block4": [(stage_x, 2, 1)],
+        3: [(stage_x, 0, 0), (stage_x, 1, 0), (stage_y, 0), (stage_y, 1)],
+        "proj_y": [(stage_x, 2, 0), (stage_y, 2)],
+        "proj_z": [(stage_x, 0, 1), (stage_x, 1, 1)],
+        "gather": [(stage_x2, 0, 0), (stage_x2, 1, 0), (stage_x2, 0, 1), (stage_x2, 1, 1),
+                   (stage_x, 2, 1), (stage_sib, 0), (stage_sib, 1)],
         "down": [(stage_x2, 2, 0), (stage_x2, 2, 1), (stage_sib, 2)],
     }
 
@@ -421,7 +420,6 @@
             a_copy(slot, ynb).wait_recv()
             a_copy(slot, ynb).start()
         if k >= LAG:
-            at_point(f"block{k - LAG}")
             zz = rem(z + order[k - LAG], nz)
             a_copy(zz * 2 + 1 - ylo, ynb).wait_recv()
             pltpu.make_async_copy(

time: 79.3 us -> 75.6 us (0.953)
  Pallas kernels: 77.7 us -> 74 us
    pallas_call x1, Pallas kernels: 75.8 us -> 72.2 us  [on_device(): pl.pallas_call(functools.partial(kernel, ncol, nx), out_shape=(jax.ShapeD...]
where the time goes in v6:
time: 75.6 us; the launch traced here: 75.5 us
  Pallas kernels  74 us (98%)
  between operations  1.45 us (2%)
    pallas_call x1, Pallas kernels, on_device(): pl.pallas_call(functools.partial(kernel, ncol, nx), out_shape=(jax.ShapeD...  72.2 us
    pallas_call x1, Pallas kernels, on_device(): pl.pallas_call(write_out, out_shape=(jax.ShapeDtypeStruct(att.shape, BF16...  1.84 us

profile of v6, /device:TPU:1, one launch (start us, length us, event | category | flops | bytes accessed | tf_op | source)
XLA Modules:
  0.0 75.5 jit_solution(15875181837685663661)
XLA Ops:
  1.3 72.2 %block.1 = (bf16[128,2048]{1,0:T(8,128)(2,1)}, bf16[128,128]{1,0:T(8,128)(2,1)}) custom-call(bf16[128,3072]{1,0:T(8,128)(2,1)} %q_h.1, bf16[32,64,576]{2,1,0:T(8,128)(2,1)} %pool_h.1, s32[32]{0:T(128)} %table_s.1, s32[32]{0:T(128)} %plen_s.1, s32[1]{0:T(128)S(6)} %copy.13.off_s, bf16[128,2048]{1,0:T(8,128)(2,1)} %hid_h.1, bf16[512,4096]{1,0:T(8,128)(2,1)} %lup_h.1, ...), custom_call_target="tpu_custom_call" | custom-call | tf_op jit(solution)/shard_map/block/pallas_call | solution.py:531
  73.5 1.8 %write_out.1 = (bf16[128,2048]{1,0:T(8,128)(2,1)}, bf16[128,128]{1,0:T(8,128)(2,1)}) custom-call(bf16[128,2048]{1,0:T(8,128)(2,1)} %get-tuple-element.4.a_h, bf16[128,128]{1,0:T(8,128)(2,1)} %get-tuple-element.5.b_h), custom_call_target="tpu_custom_call" | custom-call | tf_op jit(solution)/shard_map/write_out/pallas_call | solution.py:544

commit v7 on v6

--- a/solution.py
+++ b/solution.py
@@ -228,11 +228,12 @@
 
     plan = {
         "start": [(stage_own, 0), (stage_own, 1), (stage_own, 2)],
-        3: [(stage_x, 0, 0), (stage_x, 1, 0), (stage_y, 0), (stage_y, 1)],
-        "proj_y": [(stage_x, 2, 0), (stage_y, 2)],
+        2: [(stage_x, 0, 0), (stage_x, 1, 0)],
+        3: [(stage_y, 0), (stage_y, 1), (stage_x, 2, 0)],
+        "proj_y": [(stage_y, 2)],
         "proj_z": [(stage_x, 0, 1), (stage_x, 1, 1)],
-        "gather": [(stage_x2, 0, 0), (stage_x2, 1, 0), (stage_x2, 0, 1), (stage_x2, 1, 1),
-                   (stage_x, 2, 1), (stage_sib, 0), (stage_sib, 1)],
+        "gather": [(stage_x2, 0, 0), (stage_x2, 1, 0), (stage_x, 2, 1), (stage_x2, 0, 1), (stage_x2, 1, 1),
+                   (stage_sib, 0), (stage_sib, 1)],
         "down": [(stage_x2, 2, 0), (stage_x2, 2, 1), (stage_sib, 2)],
     }
 

time: 75.6 us -> 76.2 us (level)
  no operation moved by 1% of the time
where the time goes in v7:
time: 76.2 us; the launch traced here: 76.1 us
  Pallas kernels  74.6 us (98%)
  between operations  1.45 us (2%)
    pallas_call x1, Pallas kernels, on_device(): pl.pallas_call(functools.partial(kernel, ncol, nx), out_shape=(jax.ShapeD...  72.8 us
    pallas_call x1, Pallas kernels, on_device(): pl.pallas_call(write_out, out_shape=(jax.ShapeDtypeStruct(att.shape, BF16...  1.84 us

profile of v7, /device:TPU:1, one launch (start us, length us, event | category | flops | bytes accessed | tf_op | source)
XLA Modules:
  0.0 76.1 jit_solution(14971434956911755389)
XLA Ops:
  1.3 72.8 %block.1 = (bf16[128,2048]{1,0:T(8,128)(2,1)}, bf16[128,128]{1,0:T(8,128)(2,1)}) custom-call(bf16[128,3072]{1,0:T(8,128)(2,1)} %q_h.1, bf16[32,64,576]{2,1,0:T(8,128)(2,1)} %pool_h.1, s32[32]{0:T(128)} %table_s.1, s32[32]{0:T(128)} %plen_s.1, s32[1]{0:T(128)S(6)} %copy.13.off_s, bf16[128,2048]{1,0:T(8,128)(2,1)} %hid_h.1, bf16[512,4096]{1,0:T(8,128)(2,1)} %lup_h.1, ...), custom_call_target="tpu_custom_call" | custom-call | tf_op jit(solution)/shard_map/block/pallas_call | solution.py:532
  74.1 1.8 %write_out.1 = (bf16[128,2048]{1,0:T(8,128)(2,1)}, bf16[128,128]{1,0:T(8,128)(2,1)}) custom-call(bf16[128,2048]{1,0:T(8,128)(2,1)} %get-tuple-element.4.a_h, bf16[128,128]{1,0:T(8,128)(2,1)} %get-tuple-element.5.b_h), custom_call_target="tpu_custom_call" | custom-call | tf_op jit(solution)/shard_map/write_out/pallas_call | solution.py:545
